TPU v7x, 128 devices: a whole 4x4x4 slice. The times are simulated.
128 devices in a mesh: row: 16 (over z_lo, x, core), col: 8 (over y, z_hi).
Axes of the slice: x: 4, y: 4, z: 4 (z_hi: 2, z_lo: 2; z = z_hi * 2 + z_lo), core: 2. Of those that a mesh axis runs over, the one named last changes fastest.
Arguments:
- images: bfloat16 [4, 8, 16, 3072], P(None, 'col', 'row'), may hold values from -6 to 6
- cotangent: bfloat16 [32, 16, 4, 8, 16], P('row', None, None, 'col'), may hold values from -192 to 192
Outputs:
- kernel: float32 [32, 16, 4, 8, 16], P('row', None, None, 'col')
- image_grads: float32 [4, 8, 16, 3072], P(None, 'col', 'row')
All inputs are finite; a program needn't handle non-finite values.
Results may differ from a plain program's by a relative error of at most 0.0003.
Values may be sent and summed in bfloat16 or wider, within the bound.
A program may use at most 64 MiB of HBM per device.

v0:
```python
import math

import jax
import jax.numpy as jnp
import numpy as np
from jax import lax
from jax.sharding import PartitionSpec as P

CHAN = 3
LAYERS = 3


WEIGHT_VAR = 2.0
BIAS_VAR = 0.1


def shifted(field, offset):
    total = field.shape[-1]
    widths = [(0, 0)] * (field.ndim - 1) + [(max(-offset, 0), max(offset, 0))]
    padded = jnp.pad(field, widths)
    begin = max(offset, 0)
    return padded[..., begin : begin + total]


def spatial_blur(field, grid_side):
    column = jnp.arange(grid_side * grid_side) % grid_side
    left_ok = (column > 0).astype(jnp.float32)
    right_ok = (column < grid_side - 1).astype(jnp.float32)
    across = field + shifted(field, -1) * left_ok + shifted(field, 1) * right_ok
    summed = across + shifted(across, -grid_side) + shifted(across, grid_side)
    return WEIGHT_VAR * summed / 9.0 + BIAS_VAR


def relu_expect(cross_cov, left_var, right_var):
    fixed_cross = lax.stop_gradient(cross_cov)
    fixed_left = lax.stop_gradient(left_var)
    fixed_right = lax.stop_gradient(right_var)
    root_prod = jnp.sqrt(fixed_left * fixed_right)
    cosine = jnp.clip(fixed_cross / root_prod, -1.0, 1.0)
    angle_val = jnp.arccos(cosine)
    sine_val = jnp.sqrt(jnp.maximum(1.0 - cosine * cosine, 0.0))
    value = root_prod * (sine_val + (jnp.pi - angle_val) * cosine) / (2.0 * jnp.pi)
    slope_cross = (jnp.pi - angle_val) / (2.0 * jnp.pi)
    slope_left = jnp.sqrt(fixed_right / fixed_left) * sine_val / (4.0 * jnp.pi)
    slope_right = jnp.sqrt(fixed_left / fixed_right) * sine_val / (4.0 * jnp.pi)
    linear = slope_cross * cross_cov + slope_left * left_var + slope_right * right_var
    return lax.stop_gradient(value - linear) + linear


def tile_kernel(left_imgs, right_imgs):
    tile_rows = left_imgs.shape[0]
    positions = left_imgs.shape[1] // CHAN
    grid_side = math.isqrt(positions)
    left_px = left_imgs.reshape(tile_rows, CHAN, positions)
    right_px = right_imgs.reshape(right_imgs.shape[0], CHAN, positions)
    cross_cov = (
        jnp.einsum("acp,bcp->abp", left_px, right_px, precision=lax.Precision.HIGHEST) / CHAN
    )
    left_var = jnp.sum(left_px * left_px, axis=1) / CHAN
    right_var = jnp.sum(right_px * right_px, axis=1) / CHAN
    for layer_idx in range(LAYERS):
        cross_cov = spatial_blur(cross_cov, grid_side)
        left_var = spatial_blur(left_var, grid_side)
        right_var = spatial_blur(right_var, grid_side)
        cross_cov = relu_expect(cross_cov, left_var[:, None, :], right_var[None, :, :])
        left_var = 0.5 * left_var
        right_var = 0.5 * right_var
    return WEIGHT_VAR * jnp.mean(cross_cov, axis=-1) + BIAS_VAR


def tile_terms(left_blk, right_blk, cot_blk):
    left_full = left_blk.astype(jnp.float32)
    right_full = right_blk.astype(jnp.float32)
    value, pullback = jax.vjp(tile_kernel, left_full, right_full)
    grad_left, grad_right = pullback(cot_blk.astype(jnp.float32))
    return (value, grad_left, grad_right)


def slot_table(row_pos, col_pos, col_count, per_row):
    slot_ids = jnp.arange(2 * per_row, dtype=jnp.int32)
    upper = (2 * row_pos + slot_ids // per_row <= slot_ids % per_row * col_count + col_pos).astype(
        jnp.int32
    )
    places = jnp.cumsum(upper) - 1
    wanted = jnp.arange(2 * per_row, dtype=jnp.int32)
    hits = (upper[None, :] == 1) & (places[None, :] == wanted[:, None])
    listed = jnp.sum(jnp.where(hits, slot_ids[None, :], 0), axis=1)
    return (listed, jnp.sum(upper))


def load_table(row_count, col_count, per_row):
    row_ids = np.arange(row_count)[:, None, None, None]
    col_ids = np.arange(col_count)[None, :, None, None]
    halves = np.arange(2)[None, None, :, None]
    block_ids = np.arange(per_row)[None, None, None, :]
    return (2 * row_ids + halves <= block_ids * col_count + col_ids).sum(axis=(2, 3))


def body(images, cotangent):
    row_count = lax.axis_size("row")
    col_count = lax.axis_size("col")
    row_idx = lax.axis_index("row")
    col_idx = lax.axis_index("col")
    per_row = images.shape[0]
    feat_len = images.shape[3]
    tile_rows = images.shape[2] * row_count
    column_imgs = lax.all_gather(images, "row", axis=2, tiled=True).reshape(
        per_row, tile_rows, feat_len
    )
    own_block = 2 * row_idx // col_count
    chosen = lax.dynamic_index_in_dim(column_imgs, own_block, 0, keepdims=False)
    fetched = lax.all_gather(chosen[None], "col", axis=0, tiled=True)
    row_imgs = lax.dynamic_slice_in_dim(fetched, 2 * row_idx % col_count, 2, 0)
    cot_local = cotangent.reshape(2, tile_rows, per_row, tile_rows)
    listed, own_count = slot_table(row_idx, col_idx, col_count, per_row)
    counts = load_table(row_count, col_count, per_row)
    most_load = int(counts.max())

    def own_step(position, state):
        row_grad, col_grad, kernel_out = state
        slot = listed[position]
        live = (position < own_count).astype(jnp.float32)
        half_idx = slot // per_row
        block = slot % per_row
        left_blk = lax.dynamic_index_in_dim(row_imgs, half_idx, 0, keepdims=False)
        right_blk = lax.dynamic_index_in_dim(column_imgs, block, 0, keepdims=False)
        cot_blk = lax.dynamic_slice(
            cot_local, (half_idx, 0, block, 0), (1, tile_rows, 1, tile_rows)
        ).reshape(tile_rows, tile_rows)
        value, grad_left, grad_right = tile_terms(left_blk, right_blk, cot_blk)
        row_grad = row_grad.at[half_idx].add(grad_left * live)
        col_grad = col_grad.at[block].add(grad_right * live)
        kernel_out = kernel_out.at[half_idx, :, block, :].add(value * live)
        return (row_grad, col_grad, kernel_out)

    start = (
        jnp.zeros((2, tile_rows, feat_len), jnp.float32),
        jnp.zeros((per_row, tile_rows, feat_len), jnp.float32),
        jnp.zeros((2, tile_rows, per_row, tile_rows), jnp.float32),
    )
    row_grad, col_grad, kernel_out = lax.fori_loop(0, most_load, own_step, start)
    summed = lax.psum(row_grad, "col")
    for half_idx in range(2):
        target = (2 * row_idx + half_idx) % col_count
        match = (col_idx == target).astype(jnp.float32)
        col_grad = col_grad.at[own_block].add(summed[half_idx] * match)
    image_part = lax.psum_scatter(col_grad, "row", scatter_dimension=1, tiled=True)
    image_grads = image_part.reshape(per_row, 1, tile_rows // row_count, feat_len)
    kernel = kernel_out.reshape(2, tile_rows, per_row, 1, tile_rows)
    return (kernel, image_grads)


def solution(mesh):
    return jax.shard_map(
        body,
        mesh=mesh,
        in_specs=(P(None, "col", "row", None), P("row", None, None, "col", None)),
        out_specs=(P("row", None, None, "col", None), P(None, "col", "row", None)),
        check_vma=False,
    )
```

profile of v0, /device:TPU:1, one launch (start us, length us, event | category | flops | bytes accessed | tf_op | source)
XLA Modules:
  0.0 1035.9 jit_solution(10241776984511121998)
XLA Ops:
  7.9 22.7 %all_gather.6 = bf16[4,1,16,3072]{3,0,1,2:T(4,128)(2,1)S(1)} all-gather(bf16[4,1,1,3072]{3,0,1,2:T(4,128)(2,1)} %bitcast.70), channel_id=1, replica_groups=mesh['row'=16,'col'=8] {'row'}, dimensions={2}, use_global_device_ids=true | all-gather | bytes 417792 | tf_op jit(solution)/shard_map/all_gather | solution.py:107
  30.8 30.9 %all-gather = bf16[8,1,16,3072]{3,2,1,0:T(8,128)(2,1)S(1)} all-gather(bf16[1,1,16,3072]{3,2,1,0:T(8,128)(2,1)S(1)} %copy.65), channel_id=2, replica_groups=mesh['row'=16,'col'=8] {'col'}, dimensions={0}, use_global_device_ids=true | all-gather | bytes 884736 | tf_op jit(solution)/shard_map/all_gather | solution.py:112
  66.7 740.2 %while.27 = (s32[]{:T(128)}, f32[2,16,3072]{2,0,1:T(2,128)}, f32[4,16,3072]{2,0,1:T(4,128)}, f32[2,16,4,16]{3,2,1,0:T(4,128)}, s32[8]{0:T(128)}, /*index=5*/bf16...) while((s32[]{:T(128)}, f32[2,16,3072]{2,0,1:T(2,128)}, ...), condition=%wide.region_16.17_spmd, body=%wide.region_3.16_spmd.sunk | while | flops 71642960 | bytes 87223896 | solution.py:141
  77.5 5.4 copy.118
  94.7 5.3 multiply_reduce_fusion.9
  115.3 6.3 copy.119
  121.6 9.9 fusion.241
  138.1 4.5 scatter-add.31
  143.2 6.5 fusion.234
  170.0 5.4 copy.118
  187.3 4.9 multiply_reduce_fusion.9
  207.7 6.3 copy.119
  214.0 9.9 fusion.241
  235.6 6.5 fusion.234
  262.2 5.4 copy.118
  279.5 5.1 multiply_reduce_fusion.9
  299.9 6.3 copy.119
  306.2 9.9 fusion.241
  322.7 4.5 scatter-add.31
  327.8 6.5 fusion.234
  354.6 5.4 copy.118
  371.9 4.9 multiply_reduce_fusion.9
  392.3 6.3 copy.119
  398.6 9.9 fusion.241
  415.1 4.5 scatter-add.31
  420.2 6.5 fusion.234
  446.8 5.4 copy.118
  464.0 5.1 multiply_reduce_fusion.9
  484.4 6.3 copy.119
  490.8 9.9 fusion.241
  512.4 6.5 fusion.234
  539.2 5.4 copy.118
  556.4 4.9 multiply_reduce_fusion.9
  576.8 6.3 copy.119
  583.2 9.9 fusion.241
  604.8 6.5 fusion.234
  631.4 5.4 copy.118
  648.6 5.1 multiply_reduce_fusion.9
  669.0 6.3 copy.119
  675.3 9.9 fusion.241
  696.9 6.5 fusion.234
  723.8 5.4 copy.118
  741.0 4.9 multiply_reduce_fusion.9
  761.4 6.3 copy.119
  767.7 9.9 fusion.241
  789.3 6.5 fusion.234
  808.4 82.3 %all-reduce.76.cloned.1.call-done = f32[2,16,3072]{2,0,1:T(2,128)} async-done(((f32[2,16,3072]{2,0,1:T(2,128)}), f32[2,16,3072]{2,0,1:T(2,128)}) %all-reduce.76.cloned.1.call-update) | async-done | bytes 393232 | tf_op jit(solution)/shard_map/psum | solution.py:142
  904.8 121.9 %all-reduce.78.cloned.1.call-done = f32[4,16,3072]{2,0,1:T(4,128)} async-done(((f32[4,16,3072]{2,0,1:T(4,128)}), f32[4,16,3072]{2,0,1:T(4,128)}) %all-reduce.78.cloned.1.call-update) | async-done | bytes 786448
  (931 shorter events, 450.9 us)
Async XLA Ops:
  7.2 883.5 %all-reduce.76.cloned.1.call-start = ((), (), s32[]{:S(2)}) async-start(), calls=%async_computation | async-start | bytes 786432 | tf_op jit(solution)/shard_map/psum | solution.py:142
  30.5 32.2 %copy-start.10 = (bf16[2,16,4,1,16]{4,2,3,1,0:T(4,128)(2,1)S(1)}, bf16[2,16,4,1,16]{4,2,3,1,0:T(4,128)(2,1)}, u32[]{:S(2)}) copy-start(bf16[2,16,4,1,16]{4,2,3,1,0:T(4,128)(2,1)} %param.15) | copy-start | bytes 12292
  66.7 27.9 %copy-start.8 = (bf16[2,16,4,16]{3,1,2,0:T(8,128)(2,1)}, bf16[2,16,4,16]{3,1,2,0:T(8,128)(2,1)S(1)}, u32[]{:S(2)}) copy-start(bf16[2,16,4,16]{3,1,2,0:T(8,128)(2,1)S(1)} %get-tuple-element.778) | copy-start | bytes 12292 | tf_op jit(solution)/shard_map/while
  134.4 8.3 copy-start.5
  134.4 8.3 copy-start.6
  136.6 6.3 copy-start.4
  150.4 5.5 copy-start.13
  150.4 8.5 copy-start.9
  159.3 28.0 %copy-start.8 = (bf16[2,16,4,16]{3,1,2,0:T(8,128)(2,1)}, bf16[2,16,4,16]{3,1,2,0:T(8,128)(2,1)S(1)}, u32[]{:S(2)}) copy-start(bf16[2,16,4,16]{3,1,2,0:T(8,128)(2,1)S(1)} %get-tuple-element.778) | copy-start | bytes 12292 | tf_op jit(solution)/shard_map/while
  226.8 8.3 copy-start.5
  226.8 8.3 copy-start.6
  229.0 6.3 copy-start.4
  242.8 5.5 copy-start.13
  242.8 8.5 copy-start.9
  251.5 28.0 %copy-start.8 = (bf16[2,16,4,16]{3,1,2,0:T(8,128)(2,1)}, bf16[2,16,4,16]{3,1,2,0:T(8,128)(2,1)S(1)}, u32[]{:S(2)}) copy-start(bf16[2,16,4,16]{3,1,2,0:T(8,128)(2,1)S(1)} %get-tuple-element.778) | copy-start | bytes 12292 | tf_op jit(solution)/shard_map/while
  318.9 8.3 copy-start.5
  318.9 8.3 copy-start.6
  321.2 6.3 copy-start.4
  335.0 5.5 copy-start.13
  335.0 8.5 copy-start.9
  343.9 28.0 %copy-start.8 = (bf16[2,16,4,16]{3,1,2,0:T(8,128)(2,1)}, bf16[2,16,4,16]{3,1,2,0:T(8,128)(2,1)S(1)}, u32[]{:S(2)}) copy-start(bf16[2,16,4,16]{3,1,2,0:T(8,128)(2,1)S(1)} %get-tuple-element.778) | copy-start | bytes 12292 | tf_op jit(solution)/shard_map/while
  411.3 8.3 copy-start.5
  411.3 8.3 copy-start.6
  413.6 6.3 copy-start.4
  427.4 8.5 copy-start.9
  436.0 28.0 %copy-start.8 = (bf16[2,16,4,16]{3,1,2,0:T(8,128)(2,1)}, bf16[2,16,4,16]{3,1,2,0:T(8,128)(2,1)S(1)}, u32[]{:S(2)}) copy-start(bf16[2,16,4,16]{3,1,2,0:T(8,128)(2,1)S(1)} %get-tuple-element.778) | copy-start | bytes 12292 | tf_op jit(solution)/shard_map/while
  503.5 8.3 copy-start.5
  503.5 8.3 copy-start.6
  505.7 6.3 copy-start.4
  519.6 8.5 copy-start.9
  528.4 28.0 %copy-start.8 = (bf16[2,16,4,16]{3,1,2,0:T(8,128)(2,1)}, bf16[2,16,4,16]{3,1,2,0:T(8,128)(2,1)S(1)}, u32[]{:S(2)}) copy-start(bf16[2,16,4,16]{3,1,2,0:T(8,128)(2,1)S(1)} %get-tuple-element.778) | copy-start | bytes 12292 | tf_op jit(solution)/shard_map/while
  595.9 8.3 copy-start.5
  595.9 8.3 copy-start.6
  598.1 6.3 copy-start.4
  612.0 8.5 copy-start.9
  620.6 28.0 %copy-start.8 = (bf16[2,16,4,16]{3,1,2,0:T(8,128)(2,1)}, bf16[2,16,4,16]{3,1,2,0:T(8,128)(2,1)S(1)}, u32[]{:S(2)}) copy-start(bf16[2,16,4,16]{3,1,2,0:T(8,128)(2,1)S(1)} %get-tuple-element.778) | copy-start | bytes 12292 | tf_op jit(solution)/shard_map/while
  688.1 8.3 copy-start.5
  688.1 8.3 copy-start.6
  690.3 6.3 copy-start.4
  704.1 5.5 copy-start.13
  704.2 8.5 copy-start.9
  713.0 28.0 %copy-start.8 = (bf16[2,16,4,16]{3,1,2,0:T(8,128)(2,1)}, bf16[2,16,4,16]{3,1,2,0:T(8,128)(2,1)S(1)}, u32[]{:S(2)}) copy-start(bf16[2,16,4,16]{3,1,2,0:T(8,128)(2,1)S(1)} %get-tuple-element.778) | copy-start | bytes 12292 | tf_op jit(solution)/shard_map/while
  780.5 8.3 copy-start.5
  780.5 8.3 copy-start.6
  782.7 6.3 copy-start.4
  796.6 8.5 copy-start.9
  807.0 219.7 %all-reduce.78.cloned.1.call-start = ((), (), s32[]{:S(2)}) async-start(), calls=%async_computation.1 | async-start | bytes 1572864
  892.9 11.3 %copy-start.14 = (u32[128]{0:T(128)S(1)}, u32[128]{0:T(128)}, u32[]{:S(2)}) copy-start(u32[128]{0:T(128)} %constant.1007) | copy-start | bytes 1540
  (60 other events, 155.2 us)
Sparse Core Ops, SparseCore 0:
  807.1 83.5 all-reduce.75
  904.3 122.3 all-reduce.77
where the time goes:
time: 1040 us
  other arithmetic  296 us (28%)
  local copies, waits for them, and re-layouts  269 us (26%)
  waiting for transfers between devices  204 us (20%)
  matrix products  164 us (16%)
  blocking collectives  53.6 us (5%)
  loops' own time  34.4 us (3%)
  between operations  14.4 us (1%)
    dot_general x24, matrix products, tile_kernel(): jnp.einsum('acp,bcp->abp', left_px, right_px, precision=lax.Precision.HIG...  164 us
    unnamed x3, waiting for transfers between devices  122 us
    psum x1, waiting for transfers between devices, body(): summed = lax.psum(row_grad, 'col')  82.3 us
    reduce_sum x24, other arithmetic, relu_expect(): slope_right * right_var  68.6 us
    add x16, other arithmetic, relu_expect(): return lax.stop_gradient(value - linear) + linear  67.3 us
    dot_general x24, local copies, waits for them, and re-layouts, tile_kernel(): jnp.einsum('acp,bcp->abp', left_px, right_px, precision=lax.Precision.HIG...  62.5 us
    mul x72, other arithmetic, spatial_blur(): return WEIGHT_VAR * summed / 9.0 + BIAS_VAR  52 us
    transpose x8, local copies, waits for them, and re-layouts, tile_kernel(): jnp.einsum('acp,bcp->abp', left_px, right_px, precision=lax.Precision.HIG...  50.5 us
  transfers between devices with their start and end apart: 2, of which 2 were waited for; matrix products, arithmetic and copies ran while one was open for 0% of the time, Pallas kernels for 0%

commit v1 on v0

v1 whole, which is shorter than its diff:
```python
import math

import jax
import jax.numpy as jnp
from jax import lax
from jax.experimental import pallas as pl
from jax.experimental.pallas import tpu as pltpu
from jax.sharding import PartitionSpec as P

WEIGHT_VAR = 2.0
BIAS_VAR = 0.1
LAYERS = 3
ALPHA = [WEIGHT_VAR / 27.0]
for _ in range(LAYERS - 1):
    ALPHA.append(ALPHA[-1] * WEIGHT_VAR / 9.0)
BIAS = [BIAS_VAR / a for a in ALPHA]
ACOS = (
    1.5707957734815379,
    -0.9999221189563077,
    0.7835891615481994,
    -0.6503504235048135,
    0.5139260440580442,
    -0.3310160748218498,
    0.14106763470126799,
    -0.028090549822004016,
)
ASIN = [a / (2.0 * math.pi) for a in ACOS]
TINY = 1e-30
BATCH = 8


def lane_masks(shape):
    lane = lax.broadcasted_iota(jnp.int32, shape, len(shape) - 1)
    f = jnp.float32
    return (
        (lane % 32 != 0).astype(f),
        (lane % 32 != 31).astype(f),
        (lane >= 32).astype(f),
        (lane < 96).astype(f),
    )


def compute_kernel(n_own, n_slots, n_tiles, plan, img, cot, kout, grad, xa, ra, ta, xb, rb, tb, ub, uacc, ua, sg, sz):
    f32 = jnp.float32
    slot_count, bounds, tile_of = plan()
    left, right, upper, lower = lane_masks((16, 128))

    row3 = lax.broadcasted_iota(jnp.int32, (BATCH, 8, 128), 1)
    masks3 = lane_masks((BATCH, 8, 128))

    def image_blur(v):
        across = v + masks3[0] * pltpu.roll(v, 1, 2) + masks3[1] * pltpu.roll(v, 127, 2)
        above = pltpu.roll(across, 1, 1)
        below = pltpu.roll(across, 7, 1)
        above = jnp.where(row3 == 0, masks3[2] * pltpu.roll(above, 32, 2), above)
        below = jnp.where(row3 == 7, masks3[3] * pltpu.roll(below, 96, 2), below)
        return across + above + below

    def prologue(step, carry):
        at = pl.multiple_of(step * BATCH, BATCH)
        at8 = pl.multiple_of(step * BATCH * 8, BATCH * 8)
        val = img[pl.ds(at, BATCH)].astype(f32)
        var = jnp.zeros((BATCH, 8, 128), f32)
        for ch in range(3):
            x = val[:, ch * 8 : ch * 8 + 8, :]
            xa[ch, pl.ds(at8, BATCH * 8), :] = x.reshape(BATCH * 8, 128)
            var = var + x * x
        var = var * (1.0 / 3.0)
        for layer in range(LAYERS):
            area = (WEIGHT_VAR / 9.0) * image_blur(var) + BIAS_VAR
            inv = lax.rsqrt(area)
            ra[layer, pl.ds(at8, BATCH * 8), :] = (inv * math.sqrt(ALPHA[layer])).reshape(BATCH * 8, 128)
            ta[layer, pl.ds(at8, BATCH * 8), :] = (
                area * inv * (1.0 / math.sqrt(2.0 * math.pi * ALPHA[layer]))
            ).reshape(BATCH * 8, 128)
            var = 0.5 * area
        return carry

    batches = (n_own + slot_count + BATCH - 1) // BATCH
    lax.fori_loop(0, batches, prologue, 0)

    for group in range(n_own // 8):
        for s in range(8):
            rows = pl.ds(group * 64 + s, 8, stride=8)
            for q in range(3):
                xb[q, s, group * 8 : group * 8 + 8, :] = xa[q, rows, :]
                rb[q, s, group * 8 : group * 8 + 8, :] = ra[q, rows, :]
                tb[q, s, group * 8 : group * 8 + 8, :] = ta[q, rows, :]
    ub[...] = jnp.zeros_like(ub)
    kout[...] = jnp.zeros_like(kout)

    def across(v):
        return v + left * pltpu.roll(v, 1, 1) + right * pltpu.roll(v, 127, 1)

    def vertical(h, bias):
        top = upper * pltpu.roll(h[7], 32, 1)
        bottom = lower * pltpu.roll(h[0], 96, 1)
        if bias is not None:
            top = top + bias
            bottom = bottom + bias
        w = [None] * 8
        w[0] = (h[0] + h[1]) + top
        w[7] = (h[6] + h[7]) + bottom
        for p in (1, 3, 5):
            mid = h[p] + h[p + 1]
            if bias is not None:
                mid = mid + bias
            w[p] = h[p - 1] + mid
            w[p + 1] = mid + h[p + 2]
        return w

    lane16 = lax.broadcasted_iota(jnp.int32, (16, 128), 1)

    def slot_step(slot, carry):
        low, high = bounds(slot)
        base = (n_own + slot) * 8
        uacc[...] = jnp.zeros_like(uacc)

        def unit(bb, inner):
            own = pl.ds(pl.multiple_of(bb * 16, 16), 16)
            tile, lane = tile_of(slot, bb)

            def arow(ref, q, s):
                return ref[q, pl.ds(base + s, 1), :]

            h = []
            for s in range(8):
                x = xb[0, s, own, :] * arow(xa, 0, s)
                x = x + xb[1, s, own, :] * arow(xa, 1, s)
                x = x + xb[2, s, own, :] * arow(xa, 2, s)
                h.append(across(x))
            weight = jnp.where(lane16 == lane, cot[tile].astype(f32), 0.0)
            weight = jnp.sum(weight, axis=1, keepdims=True) * (WEIGHT_VAR * ALPHA[2] / 1024.0)
            weight = jnp.broadcast_to(weight, (16, 128))
            total = None
            for layer in range(LAYERS):
                w = vertical(h, BIAS[layer])
                h = []
                for s in range(8):
                    c = (w[s] * rb[layer, s, own, :]) * arow(ra, layer, s)
                    y = jnp.maximum(1.0 - c * c, TINY)
                    sine = y * lax.rsqrt(y)
                    poly = ASIN[7] * sine + ASIN[6]
                    for k in range(5, -1, -1):
                        poly = poly * sine + ASIN[k]
                    g = c * poly + 0.25
                    z = (sine * tb[layer, s, own, :]) * arow(ta, layer, s)
                    f = w[s] * g + z
                    if layer < LAYERS - 1:
                        sg[layer, s] = g
                        sz[layer, s] = z
                        h.append(across(f))
                    else:
                        total = f if total is None else total + f
                        e = weight * z
                        ub[layer, s, own, :] += e
                        uacc[layer, s] += e[:8] + e[8:]
                        h.append(across(weight * g))
            value = jnp.sum(total, axis=1, keepdims=True) * (WEIGHT_VAR * ALPHA[2] / 1024.0) + BIAS_VAR
            kout[tile] = jnp.where(lane16 == lane, value, kout[tile])
            for layer in range(LAYERS - 2, -1, -1):
                w = vertical(h, None)
                h = []
                for s in range(8):
                    e = w[s] * sz[layer, s]
                    ub[layer, s, own, :] += e
                    uacc[layer, s] += e[:8] + e[8:]
                    h.append(across(w[s] * sg[layer, s]))
            w = vertical(h, None)
            for s in range(8):
                for q in range(3):
                    ub[3 + q, s, own, :] += w[s] * arow(xa, q, s)
                    e = w[s] * xb[q, s, own, :]
                    uacc[3 + q, s] += e[:8] + e[8:]
            return inner

        lax.fori_loop(low, high, unit, 0)
        for k in range(6):
            for s in range(8):
                ua[k, pl.ds(base + s, 1), :] = jnp.sum(uacc[k, s], axis=0, keepdims=True)
        return carry

    lax.fori_loop(0, slot_count, slot_step, 0)

    for group in range(n_own // 8):
        for s in range(8):
            rows = pl.ds(group * 64 + s, 8, stride=8)
            for k in range(6):
                ua[k, rows, :] = ub[k, s, group * 8 : group * 8 + 8, :]

    def epilogue(step, carry):
        at = pl.multiple_of(step * BATCH, BATCH)
        at8 = pl.ds(pl.multiple_of(step * BATCH * 8, BATCH * 8), BATCH * 8)
        down = None
        for layer in range(LAYERS - 1, -1, -1):
            r = ra[layer, at8, :]
            d = ua[layer, at8, :] * (r * r) * (0.5 / ALPHA[layer])
            d = d.reshape(BATCH, 8, 128)
            if down is not None:
                d = d + 0.5 * down
            down = (WEIGHT_VAR / 9.0) * image_blur(d)
        down = down * (2.0 / 3.0)
        for q in range(3):
            x = xa[q, at8, :].reshape(BATCH, 8, 128)
            part = ua[3 + q, at8, :].reshape(BATCH, 8, 128)
            grad[pl.ds(at, BATCH), q * 8 : q * 8 + 8, :] = part + down * x
        return carry

    lax.fori_loop(0, batches, epilogue, 0)


def compute_call(n_own, n_slots, n_tiles, plan, img, cot):
    total = img.shape[0]
    vm = lambda *shape: pltpu.VMEM(shape, jnp.float32)
    whole = pl.BlockSpec(memory_space=pltpu.VMEM)

    def kernel(*refs):
        compute_kernel(n_own, n_slots, n_tiles, plan, *refs)

    return pl.pallas_call(
        kernel,
        out_shape=(
            jax.ShapeDtypeStruct((n_tiles, 16, 128), jnp.float32),
            jax.ShapeDtypeStruct((total, 24, 128), jnp.float32),
        ),
        in_specs=[whole, whole],
        out_specs=(whole, whole),
        scratch_shapes=[
            vm(3, total * 8, 128),
            vm(3, total * 8, 128),
            vm(3, total * 8, 128),
            vm(3, 8, n_own, 128),
            vm(3, 8, n_own, 128),
            vm(3, 8, n_own, 128),
            vm(6, 8, n_own, 128),
            vm(6, 8, 8, 128),
            vm(6, total * 8, 128),
            vm(2, 8, 16, 128),
            vm(2, 8, 16, 128),
        ],
        compiler_params=pltpu.CompilerParams(vmem_limit_bytes=56 * 1024 * 1024),
    )(img, cot)


def to_rows(images):
    count = images.shape[0]
    return images.reshape(count, 3, 4, 8, 32).transpose(0, 1, 3, 2, 4).reshape(count, 24, 128)


def from_rows(rows):
    count = rows.shape[0]
    return rows.reshape(count, 3, 8, 4, 32).transpose(0, 1, 3, 2, 4).reshape(count, 3072)


ROWS = 16
COLS = 8
EXTRA = 18
SLOTS = 32 + EXTRA
TABLE = 88
TILES = 6
MESH = pl.DeviceIdType.MESH


def place():
    return lax.axis_index("row"), lax.axis_index("col")


def enter(r, c):
    barrier = pltpu.get_barrier_semaphore()

    def greet(i, carry):
        rr, cc = i // COLS, i % COLS

        @pl.when(jnp.logical_or(rr != r, cc != c))
        def _():
            pl.semaphore_signal(barrier, inc=1, device_id=(rr, cc), device_id_type=MESH)

        return carry

    lax.fori_loop(0, ROWS * COLS, greet, 0)
    pl.semaphore_wait(barrier, ROWS * COLS - 1)


def send(r, c, rr, cc, src, dst, send_sem, recv_sem):
    away = jnp.logical_or(rr != r, cc != c)

    @pl.when(away)
    def _():
        pltpu.make_async_remote_copy(src, dst, send_sem, recv_sem, device_id=(rr, cc), device_id_type=MESH).start()

    @pl.when(jnp.logical_not(away))
    def _():
        pltpu.make_async_copy(src, dst, recv_sem).start()


def sent(r, c, rr, cc, src, dst, send_sem, recv_sem):
    @pl.when(jnp.logical_or(rr != r, cc != c))
    def _():
        pltpu.make_async_remote_copy(src, dst, send_sem, recv_sem, device_id=(rr, cc), device_id_type=MESH).wait_send()


def arrived(dst, recv_sem):
    pltpu.make_async_copy(dst, dst, recv_sem).wait()


def image_route(r, c, idx):
    k, m = idx // 17, idx % 17
    block = 4 * k + c // 2
    e = (c % 2) * 16 + r
    d = m % 8
    first = e < 16
    extra = m == 16
    rr = jnp.where(m < 8, block, jnp.where(extra, block + 8, block + 16 - d) % 16)
    cc = jnp.where(extra, jnp.where(first, e // 2, 0), d)
    slot = jnp.where(m < 8, e, jnp.where(extra, 64 + jnp.where(first, e % 2, e - 14), 32 + e))
    return k, rr, cc, slot


def slot_count_of(c):
    return jnp.where(c == 0, 32 + EXTRA, 34)


def cot_route(r, c, h, k):
    block, q = 4 * k + c // 2, c % 2
    dd = block - r
    straight = jnp.logical_or(dd < 8, jnp.logical_and(dd == 8, h == q))
    single = jnp.logical_and(dd >= 0, dd != 8)
    single = jnp.logical_and(single, jnp.logical_or(dd != 0, h <= q))
    rr = jnp.where(dd < 8, r, jnp.where(dd > 8, block, jnp.where(h == q, r, r + 8)))
    cc = jnp.where(dd < 8, dd, 16 - dd)
    slot = jnp.where(dd < 8, h * 2 + q, q * 2 + h)
    return dd, single, straight, rr, cc, slot


def gather_kernel(mine, cots, table, tiles, img_send, img_recv, cot_send, cot_recv, far_send):
    r, c = place()
    enter(r, c)

    def images(op):
        def step(idx, carry):
            k, rr, cc, slot = image_route(r, c, idx)
            op(r, c, rr, cc, mine.at[k], table.at[slot], img_send.at[idx], img_recv.at[slot])
            return carry

        lax.fori_loop(0, 68, step, 0)

    def tangents(op):
        def step(idx, carry):
            h, k = idx // 4, idx % 4
            dd, single, straight, rr, cc, slot = cot_route(r, c, h, k)
            turned = jnp.where(straight, 0, 8)
            src = cots.at[turned + idx]

            @pl.when(single)
            def _():
                op(r, c, rr, cc, src, tiles.at[slot], cot_send.at[idx], cot_recv.at[slot])

            @pl.when(dd == 8)
            def _():
                def far(d, inner):
                    @pl.when(jnp.logical_or(h == 0, d == 0))
                    def _():
                        op(r, c, rr, d, src, tiles.at[4 + h], far_send.at[h * 8 + d], cot_recv.at[4 + h])

                    return inner

                lax.fori_loop(0, COLS, far, 0)

            return carry

        lax.fori_loop(0, 8, step, 0)

    images(send)
    tangents(send)

    def landed(slot, carry):
        arrived(table.at[slot], img_recv.at[slot])
        return carry

    lax.fori_loop(0, 32 + slot_count_of(c), landed, 0)
    for slot in range(TILES):
        needed = (None, None, c != 0, None, None, c == 0)[slot]
        if needed is None:
            arrived(tiles.at[slot], cot_recv.at[slot])
        else:

            @pl.when(needed)
            def _():
                arrived(tiles.at[slot], cot_recv.at[slot])

    images(sent)
    tangents(sent)


def gather_call(mine, cots):
    anyspace = pl.BlockSpec(memory_space=pltpu.VMEM)
    dma = pltpu.SemaphoreType.DMA
    return pl.pallas_call(
        gather_kernel,
        out_shape=(
            jax.ShapeDtypeStruct((TABLE, 24, 128), jnp.bfloat16),
            jax.ShapeDtypeStruct((TILES, 16, 128), jnp.bfloat16),
        ),
        in_specs=[anyspace, anyspace],
        out_specs=(anyspace, anyspace),
        scratch_shapes=[dma((68,)), dma((32 + SLOTS,)), dma((8,)), dma((TILES,)), dma((16,))],
        compiler_params=pltpu.CompilerParams(collective_id=0, has_side_effects=True),
    )(mine, cots)


def partial_route(r, c, slot):
    own = slot < 32
    main = slot < 64
    n = slot - 64
    e = jnp.where(main, slot % 32, jnp.where(n < 2, 2 * c + n, 14 + n))
    block = jnp.where(own, r, jnp.where(main, r + c, r + 8) % 16)
    j = 2 * block + e // 16
    source = jnp.where(own, c, jnp.where(main, 8 + c, 16))
    return e % 16, j % 8, j // 8, source


def tile_route(r, c, slot):
    far = slot >= 4
    bb, qa = slot // 2, slot % 2
    other = jnp.where(far, (r + 8) % 16, (r + c) % 16)
    bb = jnp.where(far, jnp.where(r < 8, qa, 1 - qa), bb)
    ahead = other >= r
    i = jnp.where(ahead, 2 * r + bb, 2 * other + qa)
    j = jnp.where(ahead, 2 * other + qa, 2 * r + bb)
    return i // 2, j % 8, i % 2, j // 8


def reduce_kernel(grads, kouts, image_out, kernel_out, parts, far, part_send, part_recv, tile_send, tile_recv, far_recv):
    r, c = place()
    enter(r, c)

    def partials(op):
        def step(slot, carry):
            rr, cc, k, source = partial_route(r, c, slot)
            op(r, c, rr, cc, grads.at[slot], parts.at[k, source], part_send.at[slot], part_recv.at[k, source])
            return carry

        lax.fori_loop(0, 32 + slot_count_of(c), step, 0)

    def outputs(op):
        for slot in range(TILES):
            rr, cc, h, k = tile_route(r, c, jnp.int32(slot))
            needed = (None, None, c != 0, None, None, c == 0)[slot]
            if slot == 4:
                dst, sem = far.at[c], far_recv.at[c]
            else:
                dst, sem = kernel_out.at[h * 4 + k], tile_recv.at[h * 4 + k]
            if needed is None:
                op(r, c, rr, cc, kouts.at[slot], dst, tile_send.at[slot], sem)
            else:

                @pl.when(needed)
                def _():
                    op(r, c, rr, cc, kouts.at[slot], dst, tile_send.at[slot], sem)

    partials(send)
    outputs(send)

    for h in range(2):
        for k in range(4):
            dd, single, straight, rr, cc, slot = cot_route(r, c, h, k)
            place_ = h * 4 + k
            if h == 0:

                @pl.when(dd == 8)
                def _():
                    for d in range(COLS):
                        arrived(far.at[d], far_recv.at[d])
                    total = far[0]
                    for d in range(1, COLS):
                        total = total + far[d]
                    kernel_out[place_] = total

                get = single
            else:
                get = jnp.logical_or(single, dd == 8)

            @pl.when(get)
            def _():
                arrived(kernel_out.at[place_], tile_recv.at[place_])

            @pl.when(jnp.logical_or(dd < 0, jnp.logical_and(dd == 0, h > c % 2)))
            def _():
                kernel_out[place_] = jnp.zeros((16, 128), jnp.float32)

    for k in range(4):

        def landed(source, carry):
            arrived(parts.at[k, source], part_recv.at[k, source])
            return carry

        lax.fori_loop(0, 17, landed, 0)
        total = parts[k, 0]
        for source in range(1, 17):
            total = total + parts[k, source]
        image_out[k] = total

    partials(sent)
    outputs(sent)


def reduce_call(grads, kouts):
    whole = pl.BlockSpec(memory_space=pltpu.VMEM)
    dma = pltpu.SemaphoreType.DMA
    return pl.pallas_call(
        reduce_kernel,
        out_shape=(
            jax.ShapeDtypeStruct((4, 24, 128), jnp.float32),
            jax.ShapeDtypeStruct((8, 16, 128), jnp.float32),
        ),
        in_specs=[whole, whole],
        out_specs=(whole, whole),
        scratch_shapes=[
            pltpu.VMEM((4, 17, 24, 128), jnp.float32),
            pltpu.VMEM((8, 16, 128), jnp.float32),
            dma((32 + SLOTS,)),
            dma((4, 17)),
            dma((TILES,)),
            dma((8,)),
            dma((8,)),
        ],
        compiler_params=pltpu.CompilerParams(collective_id=1, has_side_effects=True),
    )(grads, kouts)


def plan():
    r, c = place()

    def extra(slot):
        n = slot - 32
        e = jnp.where(n < 2, 2 * c + n, 14 + n)
        return e, jnp.where(r < 8, e // 16, 1 - e // 16)

    def bounds(slot):
        e, half = extra(slot)
        main = slot < 32
        short = jnp.logical_and(c == 0, slot < 16)
        low = jnp.where(main, 0, half)
        high = jnp.where(main, jnp.where(short, 1, 2), half + 1)
        return low, high

    def tile_of(slot, bb):
        e, half = extra(slot)
        main = slot < 32
        return jnp.where(main, bb * 2 + slot // 16, 4 + e // 16), jnp.where(main, slot, e) % 16

    return slot_count_of(c), bounds, tile_of


def body(images, cotangent):
    r, c = place()
    mine = to_rows(images.reshape(4, 3072))
    cot = cotangent.reshape(2, 16, 4, 16).transpose(0, 2, 1, 3).reshape(8, 16, 16)
    cots = jnp.concatenate([cot, cot.swapaxes(1, 2)])
    cots = jnp.pad(cots, ((0, 0), (0, 0), (0, 112)))
    table, tiles = gather_call(mine, cots)
    kouts, grads = compute_call(32, SLOTS, TILES, plan, table, tiles)
    image_out, kernel_out = reduce_call(grads, kouts)
    out = kernel_out[:, :, :16].reshape(2, 4, 16, 16)
    half = jnp.arange(2)[:, None, None, None]
    k = jnp.arange(4)[None, :, None, None]
    dd = 4 * k + c // 2 - r
    straight = jnp.logical_or(dd < 8, jnp.logical_and(dd == 8, half == c % 2))
    out = jnp.where(straight, out, out.swapaxes(2, 3))
    kernel = out.transpose(0, 2, 1, 3).reshape(2, 16, 4, 1, 16)
    return kernel, from_rows(image_out).reshape(4, 1, 1, 3072)


def solution(mesh):
    return jax.shard_map(
        body,
        mesh=mesh,
        in_specs=(P(None, "col", "row", None), P("row", None, None, "col", None)),
        out_specs=(P("row", None, None, "col", None), P(None, "col", "row", None)),
        check_vma=False,
    )
```

time: 1040 us -> 147 us (0.14)
  other arithmetic: 296 us -> 2.3 us
  local copies, waits for them, and re-layouts: 269 us -> 5.88 us
  waiting for transfers between devices: 204 us -> 0 us
  matrix products: 164 us -> 0 us
  Pallas kernels: 0 us -> 137 us
  blocking collectives: 53.6 us -> 0 us
  loops' own time: 34.4 us -> 0 us
  between operations: 14.4 us -> 0.72 us
    dot_general x24 -> x0, matrix products: 164 us -> none  [tile_kernel(): jnp.einsum('acp,bcp->abp', left_px, right_px, precision=lax.Precision.HIG...]
    pallas_call x0 -> x3, Pallas kernels: none -> 137 us  [the longest x1 83.6 us: compute_call(): pl.pallas_call(kernel, out_shape=(jax.ShapeDtypeStruct((n_tiles, 16, 128)...]
    unnamed x3 -> x0, waiting for transfers between devices: 122 us -> none
    mul x304 -> x0, other arithmetic: 90.8 us -> none  [the longest x72 52 us: spatial_blur(): return WEIGHT_VAR * summed / 9.0 + BIAS_VAR]
    add x80 -> x0, other arithmetic: 86.1 us -> none  [the longest x16 67.3 us: relu_expect(): return lax.stop_gradient(value - linear) + linear]
    scatter-add x50 -> x0, local copies, waits for them, and re-layouts: 82.7 us -> none  [the longest x16 37.6 us: own_step(): col_grad = col_grad.at[block].add(grad_right * live)]
    psum x1 -> x0, waiting for transfers between devices: 82.3 us -> none  [body(): summed = lax.psum(row_grad, 'col')]
    reduce_sum x42 -> x0, other arithmetic: 70.6 us -> none  [the longest x24 68.6 us: relu_expect(): slope_right * right_var]
  transfers between devices with their start and end apart: 2 -> 0, of which waited for: 2 -> 0; matrix products, arithmetic and copies ran while one was open for 0% -> 0% of each run, Pallas kernels for 0% -> 0%
where the time goes in v1:
time: 147 us; the launch traced here: 146 us
  Pallas kernels  137 us (93%)
  local copies, waits for them, and re-layouts  5.88 us (4%)
  other arithmetic  2.3 us (2%)
    pallas_call x1, Pallas kernels, compute_call(): pl.pallas_call(kernel, out_shape=(jax.ShapeDtypeStruct((n_tiles, 16, 128)...  83.6 us
    pallas_call x1, Pallas kernels, reduce_call(): pl.pallas_call(reduce_kernel, out_shape=(jax.ShapeDtypeStruct((4, 24, 128...  27.6 us
    pallas_call x1, Pallas kernels, gather_call(): pl.pallas_call(gather_kernel, out_shape=(jax.ShapeDtypeStruct((TABLE, 24,...  26 us

profile of v1, /device:TPU:1, one launch (start us, length us, event | category | flops | bytes accessed | tf_op | source)
XLA Modules:
  0.0 146.1 jit_solution(3382022505967978045)
XLA Ops:
  0.6 0.9 reshape_reshape.6
  1.6 0.7 reshape.89.mine
  2.3 0.8 copy.5
  3.1 0.8 copy.10
  3.9 0.7 fusion.2.cots
  4.5 26.0 %shard_map.41 = (bf16[88,24,128]{2,1,0:T(8,128)(2,1)}, bf16[6,16,128]{2,1,0:T(8,128)(2,1)}) custom-call(bf16[4,24,128]{2,1,0:T(8,128)(2,1)} %reshape.89.mine, bf16[16,16,128]{2,1,0:T(8,128)(2,1)} %fusion.2.cots), custom_call_target="tpu_custom_call" | custom-call | tf_op jit(solution)/shard_map/pallas_call | solution.py:398
  30.5 83.6 %shard_map.42 = (f32[6,16,128]{2,1,0:T(8,128)}, f32[88,24,128]{2,1,0:T(8,128)}) custom-call(bf16[88,24,128]{2,1,0:T(8,128)(2,1)} %get-tuple-element.8.refs_0_, bf16[6,16,128]{2,1,0:T(8,128)(2,1)} %get-tuple-element.9.refs_1_), custom_call_target="tpu_custom_call" | custom-call | tf_op jit(solution)/shard_map/pallas_call | solution.py:220
  114.2 27.6 %shard_map.43 = (f32[4,24,128]{2,1,0:T(8,128)}, f32[8,16,128]{2,1,0:T(8,128)}) custom-call(f32[88,24,128]{2,1,0:T(8,128)} %get-tuple-element.10.grads, f32[6,16,128]{2,1,0:T(8,128)} %get-tuple-element.11.kouts), custom_call_target="tpu_custom_call" | custom-call | tf_op jit(solution)/shard_map/pallas_call | solution.py:510
  141.8 0.9 copy.7
  142.7 0.1 and_or_fusion
  142.8 1.5 %bitcast_select_fusion = f32[2,4,16,16]{3,1,2,0:T(4,128)} fusion(f32[2,4,16,16]{2,1,3,0:T(4,128)S(1)} %copy.7, f32[2,4,16,16]{3,2,1,0:T(8,128)} %bitcast.25, pred[2,4]{1,0:T(4,128)(4,1)S(1)} %and_or_fusion), kind=kLoop, calls=%fused_computation.5 | loop fusion | flops 2048 | bytes 24584 | tf_op jit(solution)/shard_map/jit(_where)/select_n | solution.py:569
  144.4 0.9 reshape.94
  145.3 0.8 reshape_reshape.7
  (4 shorter events, 0.1 us)

commit v2 on v1

--- a/solution.py
+++ b/solution.py
@@ -14,66 +14,72 @@
 for _ in range(LAYERS - 1):
     ALPHA.append(ALPHA[-1] * WEIGHT_VAR / 9.0)
 BIAS = [BIAS_VAR / a for a in ALPHA]
-ACOS = (
-    1.5707957734815379,
-    -0.9999221189563077,
-    0.7835891615481994,
-    -0.6503504235048135,
-    0.5139260440580442,
-    -0.3310160748218498,
-    0.14106763470126799,
-    -0.028090549822004016,
-)
-ASIN = [a / (2.0 * math.pi) for a in ACOS]
+ASIN = [
+    a / (2.0 * math.pi)
+    for a in (
+        -0.10520251251688581,
+        1.0690300997862225,
+        0.9916991797412131,
+        -0.4865441702586394,
+        0.1018140487237715,
+    )
+]
 TINY = 1e-30
 BATCH = 8
+HALVES = 2
 
 
 def lane_masks(shape):
     lane = lax.broadcasted_iota(jnp.int32, shape, len(shape) - 1)
     f = jnp.float32
     return (
-        (lane % 32 != 0).astype(f),
-        (lane % 32 != 31).astype(f),
-        (lane >= 32).astype(f),
-        (lane < 96).astype(f),
+        (lane % 16 != 0).astype(f),
+        (lane % 16 != 15).astype(f),
+        (lane >= 16).astype(f),
+        (lane < 112).astype(f),
     )
 
 
-def compute_kernel(n_own, n_slots, n_tiles, plan, img, cot, kout, grad, xa, ra, ta, xb, rb, tb, ub, uacc, ua, sg, sz):
+def compute_kernel(n_own, plan, img, cot, kout, grad, xa, ra, ta, xb, rb, tb, *rest):
+    ub, ua, save = rest[:6], rest[6:12], (rest[12:23], rest[23:34])
     f32 = jnp.float32
-    slot_count, bounds, tile_of = plan()
+    unit_count, slot_count, unit_of = plan()
     left, right, upper, lower = lane_masks((16, 128))
 
     row3 = lax.broadcasted_iota(jnp.int32, (BATCH, 8, 128), 1)
     masks3 = lane_masks((BATCH, 8, 128))
 
     def image_blur(v):
-        across = v + masks3[0] * pltpu.roll(v, 1, 2) + masks3[1] * pltpu.roll(v, 127, 2)
-        above = pltpu.roll(across, 1, 1)
-        below = pltpu.roll(across, 7, 1)
-        above = jnp.where(row3 == 0, masks3[2] * pltpu.roll(above, 32, 2), above)
-        below = jnp.where(row3 == 7, masks3[3] * pltpu.roll(below, 96, 2), below)
-        return across + above + below
+        even = row3 % 2 == 0
+        mate = jnp.where(even, pltpu.roll(v, 7, 1), pltpu.roll(v, 1, 1))
+        side = jnp.where(even, masks3[0] * pltpu.roll(mate, 1, 2), masks3[1] * pltpu.roll(mate, 127, 2))
+        h = v + mate + side
+        above = pltpu.roll(h, 2, 1)
+        below = pltpu.roll(h, 6, 1)
+        above = jnp.where(row3 < 2, masks3[2] * pltpu.roll(above, 16, 2), above)
+        below = jnp.where(row3 >= 6, masks3[3] * pltpu.roll(below, 112, 2), below)
+        return h + above + below
 
     def prologue(step, carry):
         at = pl.multiple_of(step * BATCH, BATCH)
-        at8 = pl.multiple_of(step * BATCH * 8, BATCH * 8)
+        at8 = pl.ds(pl.multiple_of(step * BATCH * 8, BATCH * 8), BATCH * 8)
         val = img[pl.ds(at, BATCH)].astype(f32)
         var = jnp.zeros((BATCH, 8, 128), f32)
         for ch in range(3):
             x = val[:, ch * 8 : ch * 8 + 8, :]
-            xa[ch, pl.ds(at8, BATCH * 8), :] = x.reshape(BATCH * 8, 128)
+            xa[ch, at8, :] = x.reshape(BATCH * 8, 128)
             var = var + x * x
         var = var * (1.0 / 3.0)
         for layer in range(LAYERS):
             area = (WEIGHT_VAR / 9.0) * image_blur(var) + BIAS_VAR
             inv = lax.rsqrt(area)
-            ra[layer, pl.ds(at8, BATCH * 8), :] = (inv * math.sqrt(ALPHA[layer])).reshape(BATCH * 8, 128)
-            ta[layer, pl.ds(at8, BATCH * 8), :] = (
+            ra[layer, at8, :] = (inv * math.sqrt(ALPHA[layer])).reshape(BATCH * 8, 128)
+            ta[layer, at8, :] = (
                 area * inv * (1.0 / math.sqrt(2.0 * math.pi * ALPHA[layer]))
             ).reshape(BATCH * 8, 128)
             var = 0.5 * area
+        for k in range(6):
+            ua[k][at8, :] = jnp.zeros((BATCH * 8, 128), f32)
         return carry
 
     batches = (n_own + slot_count + BATCH - 1) // BATCH
@@ -82,111 +88,143 @@
     for group in range(n_own // 8):
         for s in range(8):
             rows = pl.ds(group * 64 + s, 8, stride=8)
+            part = slice(group * 8, group * 8 + 8)
             for q in range(3):
-                xb[q, s, group * 8 : group * 8 + 8, :] = xa[q, rows, :]
-                rb[q, s, group * 8 : group * 8 + 8, :] = ra[q, rows, :]
-                tb[q, s, group * 8 : group * 8 + 8, :] = ta[q, rows, :]
-    ub[...] = jnp.zeros_like(ub)
+                xb[q, s, part, :] = xa[q, rows, :]
+                rb[q, s, part, :] = ra[q, rows, :]
+                tb[q, s, part, :] = ta[q, rows, :]
+    for k in range(6):
+        ub[k][...] = jnp.zeros_like(ub[k])
     kout[...] = jnp.zeros_like(kout)
 
     def across(v):
-        return v + left * pltpu.roll(v, 1, 1) + right * pltpu.roll(v, 127, 1)
+        out = [None] * 8
+        for p in range(0, 8, 2):
+            mid = v[p] + v[p + 1]
+            out[p] = mid + left * pltpu.roll(v[p + 1], 1, 1)
+            out[p + 1] = mid + right * pltpu.roll(v[p], 127, 1)
+        return out
 
     def vertical(h, bias):
-        top = upper * pltpu.roll(h[7], 32, 1)
-        bottom = lower * pltpu.roll(h[0], 96, 1)
-        if bias is not None:
-            top = top + bias
-            bottom = bottom + bias
         w = [None] * 8
-        w[0] = (h[0] + h[1]) + top
-        w[7] = (h[6] + h[7]) + bottom
-        for p in (1, 3, 5):
-            mid = h[p] + h[p + 1]
+        for sx in range(2):
+            top = upper * pltpu.roll(h[6 + sx], 16, 1)
+            bottom = lower * pltpu.roll(h[sx], 112, 1)
+            one = h[sx] + h[2 + sx]
+            two = h[4 + sx] + h[6 + sx]
             if bias is not None:
-                mid = mid + bias
-            w[p] = h[p - 1] + mid
-            w[p + 1] = mid + h[p + 2]
+                one = one + bias
+                two = two + bias
+            w[sx] = one + top
+            w[2 + sx] = one + h[4 + sx]
+            w[4 + sx] = h[2 + sx] + two
+            w[6 + sx] = two + bottom
         return w
 
     lane16 = lax.broadcasted_iota(jnp.int32, (16, 128), 1)
-
-    def slot_step(slot, carry):
-        low, high = bounds(slot)
-        base = (n_own + slot) * 8
-        uacc[...] = jnp.zeros_like(uacc)
-
-        def unit(bb, inner):
-            own = pl.ds(pl.multiple_of(bb * 16, 16), 16)
-            tile, lane = tile_of(slot, bb)
-
-            def arow(ref, q, s):
-                return ref[q, pl.ds(base + s, 1), :]
-
-            h = []
-            for s in range(8):
-                x = xb[0, s, own, :] * arow(xa, 0, s)
-                x = x + xb[1, s, own, :] * arow(xa, 1, s)
-                x = x + xb[2, s, own, :] * arow(xa, 2, s)
-                h.append(across(x))
-            weight = jnp.where(lane16 == lane, cot[tile].astype(f32), 0.0)
-            weight = jnp.sum(weight, axis=1, keepdims=True) * (WEIGHT_VAR * ALPHA[2] / 1024.0)
-            weight = jnp.broadcast_to(weight, (16, 128))
-            total = None
-            for layer in range(LAYERS):
-                w = vertical(h, BIAS[layer])
-                h = []
-                for s in range(8):
-                    c = (w[s] * rb[layer, s, own, :]) * arow(ra, layer, s)
-                    y = jnp.maximum(1.0 - c * c, TINY)
-                    sine = y * lax.rsqrt(y)
-                    poly = ASIN[7] * sine + ASIN[6]
-                    for k in range(5, -1, -1):
-                        poly = poly * sine + ASIN[k]
-                    g = c * poly + 0.25
-                    z = (sine * tb[layer, s, own, :]) * arow(ta, layer, s)
-                    f = w[s] * g + z
-                    if layer < LAYERS - 1:
-                        sg[layer, s] = g
-                        sz[layer, s] = z
-                        h.append(across(f))
-                    else:
-                        total = f if total is None else total + f
-                        e = weight * z
-                        ub[layer, s, own, :] += e
-                        uacc[layer, s] += e[:8] + e[8:]
-                        h.append(across(weight * g))
-            value = jnp.sum(total, axis=1, keepdims=True) * (WEIGHT_VAR * ALPHA[2] / 1024.0) + BIAS_VAR
-            kout[tile] = jnp.where(lane16 == lane, value, kout[tile])
-            for layer in range(LAYERS - 2, -1, -1):
-                w = vertical(h, None)
-                h = []
-                for s in range(8):
-                    e = w[s] * sz[layer, s]
-                    ub[layer, s, own, :] += e
-                    uacc[layer, s] += e[:8] + e[8:]
-                    h.append(across(w[s] * sg[layer, s]))
+    ORDER = (0, 7, 1, 6, 2, 5, 3, 4)
+
+    def ready(u):
+        live = u < unit_count
+        slot, bb, tile, lane = unit_of(jnp.minimum(u, unit_count - 1))
+        base = pl.multiple_of((n_own + slot) * 8, 8)
+        own = pl.ds(pl.multiple_of(bb * 16, 16), 16)
+        return live, base, own, tile, lane
+
+    def arow(ref, q, base, s):
+        return ref[q, pl.ds(base + s, 1), :]
+
+    def fold(uacc, k, base):
+        total = uacc[k][pl.ds(0, 8, stride=8), :]
+        for b in range(1, 8):
+            total = total + uacc[k][pl.ds(b, 8, stride=8), :]
+        ua[k][pl.ds(base, 8), :] += total
+
+    def tally(uacc, k, s, own, e_own, e_slot):
+        ub[k][s, own, :] += e_own
+        uacc[k][s * 8 : s * 8 + 8, :] = e_slot[:8] + e_slot[8:]
+
+    def forward(u, saved):
+        sg1, sz1, sg2, sz2, sh, *uacc = saved
+        live, base, own, tile, lane = ready(u)
+        h = [None] * 8
+        for s in ORDER:
+            x = xb[0, s, own, :] * arow(xa, 0, base, s)
+            x = x + xb[1, s, own, :] * arow(xa, 1, base, s)
+            x = x + xb[2, s, own, :] * arow(xa, 2, base, s)
+            h[s] = x
+        h = across(h)
+        weight = jnp.where(lane16 == lane, cot[tile].astype(f32), 0.0)
+        weight = jnp.sum(weight, axis=1, keepdims=True) * (WEIGHT_VAR * ALPHA[2] / 1024.0)
+        weight = jnp.where(live, jnp.broadcast_to(weight, (16, 128)), 0.0)
+        total = None
+        for layer in range(LAYERS):
+            w = vertical(h, BIAS[layer])
+            h = [None] * 8
+            for s in ORDER:
+                c = (w[s] * rb[layer, s, own, :]) * arow(ra, layer, base, s)
+                y = jnp.maximum(1.0 - c * c, TINY)
+                sine = y * lax.rsqrt(y)
+                v = lax.rsqrt(1.0 + sine)
+                poly = ASIN[4] * v + ASIN[3]
+                for k in range(2, -1, -1):
+                    poly = poly * v + ASIN[k]
+                g = c * poly + 0.25
+                z = (sine * tb[layer, s, own, :]) * arow(ta, layer, base, s)
+                f = w[s] * g + z
+                if layer < LAYERS - 1:
+                    (sg1, sg2)[layer][s] = g
+                    (sz1, sz2)[layer][s] = z
+                    h[s] = f
+                else:
+                    total = f if total is None else total + f
+                    e = weight * z
+                    tally(uacc, layer, s, own, e, e)
+                    h[s] = weight * g
+            h = across(h)
+        for s in range(8):
+            sh[s] = h[s]
+        fold(uacc, LAYERS - 1, base)
+        value = jnp.sum(total, axis=1, keepdims=True) * (WEIGHT_VAR * ALPHA[2] / 1024.0) + BIAS_VAR
+        kout[tile] = jnp.where(lane16 == lane, value, kout[tile])
+
+    def backward(u, saved):
+        sg1, sz1, sg2, sz2, sh, *uacc = saved
+        live, base, own, tile, lane = ready(u)
+        h = [sh[s] for s in range(8)]
+        for layer in range(LAYERS - 2, -1, -1):
             w = vertical(h, None)
-            for s in range(8):
-                for q in range(3):
-                    ub[3 + q, s, own, :] += w[s] * arow(xa, q, s)
-                    e = w[s] * xb[q, s, own, :]
-                    uacc[3 + q, s] += e[:8] + e[8:]
-            return inner
-
-        lax.fori_loop(low, high, unit, 0)
-        for k in range(6):
-            for s in range(8):
-                ua[k, pl.ds(base + s, 1), :] = jnp.sum(uacc[k, s], axis=0, keepdims=True)
+            h = [None] * 8
+            for s in ORDER:
+                e = w[s] * (sz1, sz2)[layer][s]
+                tally(uacc, layer, s, own, e, e)
+                h[s] = w[s] * (sg1, sg2)[layer][s]
+            h = across(h)
+            fold(uacc, layer, base)
+        w = vertical(h, None)
+        for s in range(8):
+            for q in range(3):
+                tally(uacc, 3 + q, s, own, w[s] * arow(xa, q, base, s), w[s] * xb[q, s, own, :])
+        for q in range(3):
+            fold(uacc, 3 + q, base)
+
+    forward(jnp.int32(0), save[0])
+    forward(jnp.int32(1), save[1])
+
+    def pair(i, carry):
+        backward(2 * i, save[0])
+        forward(2 * i + 2, save[0])
+        backward(2 * i + 1, save[1])
+        forward(2 * i + 3, save[1])
         return carry
 
-    lax.fori_loop(0, slot_count, slot_step, 0)
+    lax.fori_loop(0, unit_count // 2, pair, 0)
 
     for group in range(n_own // 8):
         for s in range(8):
             rows = pl.ds(group * 64 + s, 8, stride=8)
             for k in range(6):
-                ua[k, rows, :] = ub[k, s, group * 8 : group * 8 + 8, :]
+                ua[k][rows, :] = ub[k][s, group * 8 : group * 8 + 8, :]
 
     def epilogue(step, carry):
         at = pl.multiple_of(step * BATCH, BATCH)
@@ -194,7 +232,7 @@
         down = None
         for layer in range(LAYERS - 1, -1, -1):
             r = ra[layer, at8, :]
-            d = ua[layer, at8, :] * (r * r) * (0.5 / ALPHA[layer])
+            d = ua[layer][at8, :] * (r * r) * (0.5 / ALPHA[layer])
             d = d.reshape(BATCH, 8, 128)
             if down is not None:
                 d = d + 0.5 * down
@@ -202,20 +240,20 @@
         down = down * (2.0 / 3.0)
         for q in range(3):
             x = xa[q, at8, :].reshape(BATCH, 8, 128)
-            part = ua[3 + q, at8, :].reshape(BATCH, 8, 128)
+            part = ua[3 + q][at8, :].reshape(BATCH, 8, 128)
             grad[pl.ds(at, BATCH), q * 8 : q * 8 + 8, :] = part + down * x
         return carry
 
     lax.fori_loop(0, batches, epilogue, 0)
 
 
-def compute_call(n_own, n_slots, n_tiles, plan, img, cot):
+def compute_call(n_own, n_tiles, plan, img, cot):
     total = img.shape[0]
     vm = lambda *shape: pltpu.VMEM(shape, jnp.float32)
     whole = pl.BlockSpec(memory_space=pltpu.VMEM)
 
     def kernel(*refs):
-        compute_kernel(n_own, n_slots, n_tiles, plan, *refs)
+        compute_kernel(n_own, plan, *refs)
 
     return pl.pallas_call(
         kernel,
@@ -225,31 +263,23 @@
         ),
         in_specs=[whole, whole],
         out_specs=(whole, whole),
-        scratch_shapes=[
-            vm(3, total * 8, 128),
-            vm(3, total * 8, 128),
-            vm(3, total * 8, 128),
-            vm(3, 8, n_own, 128),
-            vm(3, 8, n_own, 128),
-            vm(3, 8, n_own, 128),
-            vm(6, 8, n_own, 128),
-            vm(6, 8, 8, 128),
-            vm(6, total * 8, 128),
-            vm(2, 8, 16, 128),
-            vm(2, 8, 16, 128),
-        ],
+        scratch_shapes=[vm(3, total * 8, 128)] * 3
+        + [vm(3, 8, n_own, 128)] * 3
+        + [vm(8, n_own, 128)] * 6
+        + [vm(total * 8, 128)] * 6
+        + ([vm(8, 16, 128)] * 5 + [vm(64, 128)] * 6) * 2,
         compiler_params=pltpu.CompilerParams(vmem_limit_bytes=56 * 1024 * 1024),
     )(img, cot)
 
 
 def to_rows(images):
     count = images.shape[0]
-    return images.reshape(count, 3, 4, 8, 32).transpose(0, 1, 3, 2, 4).reshape(count, 24, 128)
+    return images.reshape(count, 3, 8, 4, 16, 2).transpose(0, 1, 3, 5, 2, 4).reshape(count, 24, 128)
 
 
 def from_rows(rows):
     count = rows.shape[0]
-    return rows.reshape(count, 3, 8, 4, 32).transpose(0, 1, 3, 2, 4).reshape(count, 3072)
+    return rows.reshape(count, 3, 4, 2, 8, 16).transpose(0, 1, 4, 2, 5, 3).reshape(count, 3072)
 
 
 ROWS = 16
@@ -531,25 +561,20 @@
 def plan():
     r, c = place()
 
-    def extra(slot):
-        n = slot - 32
+    def unit_of(u):
+        first = c == 0
+        n = u - jnp.where(first, 48, 64)
+        main = n < 0
         e = jnp.where(n < 2, 2 * c + n, 14 + n)
-        return e, jnp.where(r < 8, e // 16, 1 - e // 16)
-
-    def bounds(slot):
-        e, half = extra(slot)
-        main = slot < 32
-        short = jnp.logical_and(c == 0, slot < 16)
-        low = jnp.where(main, 0, half)
-        high = jnp.where(main, jnp.where(short, 1, 2), half + 1)
-        return low, high
-
-    def tile_of(slot, bb):
-        e, half = extra(slot)
-        main = slot < 32
-        return jnp.where(main, bb * 2 + slot // 16, 4 + e // 16), jnp.where(main, slot, e) % 16
-
-    return slot_count_of(c), bounds, tile_of
+        half = jnp.where(r < 8, e // 16, 1 - e // 16)
+        short = jnp.logical_and(first, u < 16)
+        v = jnp.where(first, u + 16, u)
+        slot = jnp.where(main, jnp.where(short, u, v // 2), 32 + n)
+        bb = jnp.where(main, jnp.where(short, 0, v % 2), half)
+        tile = jnp.where(main, bb * 2 + slot // 16, 4 + e // 16)
+        return slot, bb, tile, jnp.where(main, slot, e) % 16
+
+    return 66, slot_count_of(c), unit_of
 
 
 def body(images, cotangent):
@@ -559,7 +584,7 @@
     cots = jnp.concatenate([cot, cot.swapaxes(1, 2)])
     cots = jnp.pad(cots, ((0, 0), (0, 0), (0, 112)))
     table, tiles = gather_call(mine, cots)
-    kouts, grads = compute_call(32, SLOTS, TILES, plan, table, tiles)
+    kouts, grads = compute_call(32, TILES, plan, table, tiles)
     image_out, kernel_out = reduce_call(grads, kouts)
     out = kernel_out[:, :, :16].reshape(2, 4, 16, 16)
     half = jnp.arange(2)[:, None, None, None]

time: 147 us -> 112 us (0.76)
  Pallas kernels: 137 us -> 98.6 us
  local copies, waits for them, and re-layouts: 5.88 us -> 9.7 us
    pallas_call x1, Pallas kernels: 83.6 us -> 45.2 us  [compute_call(): pl.pallas_call(kernel, out_shape=(jax.ShapeDtypeStruct((n_tiles, 16, 128)...]
    unnamed x0 -> x2, local copies, waits for them, and re-layouts: none -> 2.25 us
    transpose x1, local copies, waits for them, and re-layouts: 0.01 us -> 1.76 us  [to_rows(): images.reshape(count, 3, 8, 4, 16, 2).transpose(0, 1, 3, 5, 2, 4)]
    another operation x3 -> x0, local copies, waits for them, and re-layouts: 1.67 us -> none  [the longest x2 0.91 us: to_rows(): images.reshape(count, 3, 4, 8, 32).transpose(0, 1, 3, 2, 4)]
    reshape x2 -> x3, local copies, waits for them, and re-layouts: 1.66 us -> 3.16 us  [the longest x2 2.39 us: from_rows(): rows.reshape(count, 3, 4, 2, 8, 16).transpose(0, 1, 4, 2, 5, 3)]
where the time goes in v2:
time: 112 us; the launch traced here: 111 us
  Pallas kernels  98.6 us (88%)
  local copies, waits for them, and re-layouts  9.7 us (9%)
  other arithmetic  2.3 us (2%)
    pallas_call x1, Pallas kernels, compute_call(): pl.pallas_call(kernel, out_shape=(jax.ShapeDtypeStruct((n_tiles, 16, 128)...  45.2 us
    pallas_call x1, Pallas kernels, reduce_call(): pl.pallas_call(reduce_kernel, out_shape=(jax.ShapeDtypeStruct((4, 24, 128...  27.4 us
    pallas_call x1, Pallas kernels, gather_call(): pl.pallas_call(gather_kernel, out_shape=(jax.ShapeDtypeStruct((TABLE, 24,...  26 us
    reshape x2, local copies, waits for them, and re-layouts, from_rows(): rows.reshape(count, 3, 4, 2, 8, 16).transpose(0, 1, 4, 2, 5, 3)  2.39 us
    unnamed x2, local copies, waits for them, and re-layouts  2.25 us

profile of v2, /device:TPU:1, one launch (start us, length us, event | category | flops | bytes accessed | tf_op | source)
XLA Modules:
  0.0 111.3 jit_solution(16974672440578731650)
XLA Ops:
  0.7 0.1 and_or_fusion
  0.8 0.8 copy.18
  1.5 0.8 copy.12
  2.4 0.7 fusion.2.cots
  3.0 1.2 %copy.10 = bf16[4,1,1,3072]{0,3,2,1:T(8,128)(2,1)S(1)} copy(bf16[4,1,1,3072]{3,0,2,1:T(4,128)(2,1)} %param.2) | data formatting | bytes 49152 | tf_op args[0]
  4.2 1.8 %copy.11 = bf16[4,3,4,2,8,16]{5,4,3,2,1,0:T(8,128)(2,1)S(1)} copy(bf16[4,3,4,2,8,16]{0,3,5,2,4,1:T(2,128)(2,1)S(1)} %bitcast.23) | data formatting | bytes 49152 | tf_op jit(solution)/shard_map/transpose | solution.py:277
  6.0 0.8 reshape.89.mine
  6.7 26.0 %shard_map.41 = (bf16[88,24,128]{2,1,0:T(8,128)(2,1)}, bf16[6,16,128]{2,1,0:T(8,128)(2,1)}) custom-call(bf16[4,24,128]{2,1,0:T(8,128)(2,1)} %reshape.89.mine, bf16[16,16,128]{2,1,0:T(8,128)(2,1)} %fusion.2.cots), custom_call_target="tpu_custom_call" | custom-call | tf_op jit(solution)/shard_map/pallas_call | solution.py:428
  32.7 45.2 %shard_map.42 = (f32[6,16,128]{2,1,0:T(8,128)}, f32[88,24,128]{2,1,0:T(8,128)}) custom-call(bf16[88,24,128]{2,1,0:T(8,128)(2,1)} %get-tuple-element.8.refs_0_, bf16[6,16,128]{2,1,0:T(8,128)(2,1)} %get-tuple-element.9.refs_1_), custom_call_target="tpu_custom_call" | custom-call | tf_op jit(solution)/shard_map/pallas_call | solution.py:258
  77.9 27.4 %shard_map.43 = (f32[4,24,128]{2,1,0:T(8,128)}, f32[8,16,128]{2,1,0:T(8,128)}) custom-call(f32[88,24,128]{2,1,0:T(8,128)} %get-tuple-element.10.grads, f32[6,16,128]{2,1,0:T(8,128)} %get-tuple-element.11.kouts), custom_call_target="tpu_custom_call" | custom-call | tf_op jit(solution)/shard_map/pallas_call | solution.py:540
  105.4 0.9 copy.14
  106.3 1.6 %bitcast_select_fusion = f32[2,4,16,16]{3,1,2,0:T(4,128)} fusion(f32[2,4,16,16]{2,1,3,0:T(4,128)S(1)} %copy.14, f32[2,4,16,16]{3,2,1,0:T(8,128)} %bitcast.25, pred[2,4]{1,0:T(4,128)(4,1)S(1)} %and_or_fusion), kind=kLoop, calls=%fused_computation.4 | loop fusion | flops 2048 | bytes 24584 | tf_op jit(solution)/shard_map/jit(_where)/select_n | solution.py:594
  107.8 0.9 reshape.94
  108.8 1.4 %copy.16 = f32[4,3,4,2,8,16]{0,3,5,2,4,1:T(2,128)S(1)} copy(f32[4,3,4,2,8,16]{5,4,3,2,1,0:T(8,128)S(1)} %reshape.94) | data formatting | bytes 98304 | tf_op jit(solution)/shard_map/reshape | solution.py:282
  110.2 1.1 copy.17
  (2 shorter events, 0.0 us)

commit v3 on v2

--- a/solution.py
+++ b/solution.py
@@ -247,31 +247,6 @@
     lax.fori_loop(0, batches, epilogue, 0)
 
 
-def compute_call(n_own, n_tiles, plan, img, cot):
-    total = img.shape[0]
-    vm = lambda *shape: pltpu.VMEM(shape, jnp.float32)
-    whole = pl.BlockSpec(memory_space=pltpu.VMEM)
-
-    def kernel(*refs):
-        compute_kernel(n_own, plan, *refs)
-
-    return pl.pallas_call(
-        kernel,
-        out_shape=(
-            jax.ShapeDtypeStruct((n_tiles, 16, 128), jnp.float32),
-            jax.ShapeDtypeStruct((total, 24, 128), jnp.float32),
-        ),
-        in_specs=[whole, whole],
-        out_specs=(whole, whole),
-        scratch_shapes=[vm(3, total * 8, 128)] * 3
-        + [vm(3, 8, n_own, 128)] * 3
-        + [vm(8, n_own, 128)] * 6
-        + [vm(total * 8, 128)] * 6
-        + ([vm(8, 16, 128)] * 5 + [vm(64, 128)] * 6) * 2,
-        compiler_params=pltpu.CompilerParams(vmem_limit_bytes=56 * 1024 * 1024),
-    )(img, cot)
-
-
 def to_rows(images):
     count = images.shape[0]
     return images.reshape(count, 3, 8, 4, 16, 2).transpose(0, 1, 3, 5, 2, 4).reshape(count, 24, 128)
@@ -297,53 +272,59 @@
 
 def enter(r, c):
     barrier = pltpu.get_barrier_semaphore()
-
-    def greet(i, carry):
-        rr, cc = i // COLS, i % COLS
-
-        @pl.when(jnp.logical_or(rr != r, cc != c))
-        def _():
-            pl.semaphore_signal(barrier, inc=1, device_id=(rr, cc), device_id_type=MESH)
-
-        return carry
-
-    lax.fori_loop(0, ROWS * COLS, greet, 0)
+    me = r * COLS + c
+    for i in range(1, ROWS * COLS):
+        peer = (me + i) & (ROWS * COLS - 1)
+        pl.semaphore_signal(barrier, inc=1, device_id=(peer >> 3, peer & 7), device_id_type=MESH)
     pl.semaphore_wait(barrier, ROWS * COLS - 1)
 
 
-def send(r, c, rr, cc, src, dst, send_sem, recv_sem):
-    away = jnp.logical_or(rr != r, cc != c)
-
-    @pl.when(away)
+def ship(go, away, rr, cc, src, dst, send_sem, recv_sem):
+    def remote():
+        pltpu.make_async_remote_copy(src, dst, send_sem, recv_sem, device_id=(rr, cc), device_id_type=MESH).start()
+
+    def local():
+        pltpu.make_async_copy(src, dst, recv_sem).start()
+
+    guarded(go, away, remote)
+    if away is not None:
+        guarded(go, jnp.logical_not(away), local)
+
+
+def shipped(go, away, rr, cc, src, dst, send_sem, recv_sem):
+    guarded(go, away, lambda: pltpu.make_async_copy(src, src, send_sem).wait())
+
+
+def guarded(one, two, work):
+    conds = [x for x in (one, two) if x is not None]
+    if not conds:
+        work()
+        return
+    cond = conds[0] if len(conds) == 1 else jnp.logical_and(*conds)
+
+    @pl.when(cond)
     def _():
-        pltpu.make_async_remote_copy(src, dst, send_sem, recv_sem, device_id=(rr, cc), device_id_type=MESH).start()
-
-    @pl.when(jnp.logical_not(away))
-    def _():
-        pltpu.make_async_copy(src, dst, recv_sem).start()
-
-
-def sent(r, c, rr, cc, src, dst, send_sem, recv_sem):
-    @pl.when(jnp.logical_or(rr != r, cc != c))
-    def _():
-        pltpu.make_async_remote_copy(src, dst, send_sem, recv_sem, device_id=(rr, cc), device_id_type=MESH).wait_send()
+        work()
 
 
 def arrived(dst, recv_sem):
     pltpu.make_async_copy(dst, dst, recv_sem).wait()
 
 
-def image_route(r, c, idx):
-    k, m = idx // 17, idx % 17
-    block = 4 * k + c // 2
-    e = (c % 2) * 16 + r
-    d = m % 8
-    first = e < 16
-    extra = m == 16
-    rr = jnp.where(m < 8, block, jnp.where(extra, block + 8, block + 16 - d) % 16)
-    cc = jnp.where(extra, jnp.where(first, e // 2, 0), d)
-    slot = jnp.where(m < 8, e, jnp.where(extra, 64 + jnp.where(first, e % 2, e - 14), 32 + e))
-    return k, rr, cc, slot
+def image_routes(r, c):
+    e = ((c & 1) << 4) + r
+    early = e < 16
+    for k in range(4):
+        block = 4 * k + (c >> 1)
+        for i in range(COLS):
+            d = (c + i) & 7
+            yield k, block, d, e, (block != r if i == 0 else None)
+            rr = (block + 16 - d) & 15
+            yield k, rr, d, 32 + e, (rr != r if i == 0 else None)
+        rr = (block + 8) & 15
+        d = jnp.where(early, e >> 1, 0)
+        slot = jnp.where(early, 64 + (e & 1), 50 + e)
+        yield k, rr, d, slot, jnp.logical_or(rr != r, d != c)
 
 
 def slot_count_of(c):
@@ -351,150 +332,132 @@
 
 
 def cot_route(r, c, h, k):
-    block, q = 4 * k + c // 2, c % 2
+    q = c & 1
+    block = 4 * k + (c >> 1)
     dd = block - r
-    straight = jnp.logical_or(dd < 8, jnp.logical_and(dd == 8, h == q))
+    straight = jnp.logical_or(dd < 8, jnp.logical_and(dd == 8, q == h))
     single = jnp.logical_and(dd >= 0, dd != 8)
-    single = jnp.logical_and(single, jnp.logical_or(dd != 0, h <= q))
-    rr = jnp.where(dd < 8, r, jnp.where(dd > 8, block, jnp.where(h == q, r, r + 8)))
-    cc = jnp.where(dd < 8, dd, 16 - dd)
-    slot = jnp.where(dd < 8, h * 2 + q, q * 2 + h)
+    if h == 1:
+        single = jnp.logical_and(single, jnp.logical_or(dd != 0, q == 1))
+    near = dd < 8
+    rr = jnp.where(near, r, block)
+    cc = jnp.where(near, dd, 16 - dd) & 7
+    slot = jnp.where(near, h * 2 + q, q * 2 + h)
     return dd, single, straight, rr, cc, slot
 
 
-def gather_kernel(mine, cots, table, tiles, img_send, img_recv, cot_send, cot_recv, far_send):
-    r, c = place()
-    enter(r, c)
-
-    def images(op):
-        def step(idx, carry):
-            k, rr, cc, slot = image_route(r, c, idx)
-            op(r, c, rr, cc, mine.at[k], table.at[slot], img_send.at[idx], img_recv.at[slot])
-            return carry
-
-        lax.fori_loop(0, 68, step, 0)
-
-    def tangents(op):
-        def step(idx, carry):
-            h, k = idx // 4, idx % 4
+def tangents(op, r, c, cots, tiles, cot_send, cot_recv, far_send):
+    for h in range(2):
+        for k in range(4):
+            idx = h * 4 + k
             dd, single, straight, rr, cc, slot = cot_route(r, c, h, k)
-            turned = jnp.where(straight, 0, 8)
-            src = cots.at[turned + idx]
-
-            @pl.when(single)
-            def _():
-                op(r, c, rr, cc, src, tiles.at[slot], cot_send.at[idx], cot_recv.at[slot])
+            src = cots.at[jnp.where(straight, idx, 8 + idx)]
+            op(single, dd != c, rr, cc, src, tiles.at[slot], cot_send.at[idx], cot_recv.at[slot])
 
             @pl.when(dd == 8)
             def _():
-                def far(d, inner):
-                    @pl.when(jnp.logical_or(h == 0, d == 0))
-                    def _():
-                        op(r, c, rr, d, src, tiles.at[4 + h], far_send.at[h * 8 + d], cot_recv.at[4 + h])
-
-                    return inner
-
-                lax.fori_loop(0, COLS, far, 0)
-
-            return carry
-
-        lax.fori_loop(0, 8, step, 0)
-
-    images(send)
-    tangents(send)
-
-    def landed(slot, carry):
-        arrived(table.at[slot], img_recv.at[slot])
-        return carry
-
-    lax.fori_loop(0, 32 + slot_count_of(c), landed, 0)
-    for slot in range(TILES):
-        needed = (None, None, c != 0, None, None, c == 0)[slot]
-        if needed is None:
-            arrived(tiles.at[slot], cot_recv.at[slot])
-        else:
-
-            @pl.when(needed)
-            def _():
-                arrived(tiles.at[slot], cot_recv.at[slot])
-
-    images(sent)
-    tangents(sent)
-
-
-def gather_call(mine, cots):
-    anyspace = pl.BlockSpec(memory_space=pltpu.VMEM)
-    dma = pltpu.SemaphoreType.DMA
-    return pl.pallas_call(
-        gather_kernel,
-        out_shape=(
-            jax.ShapeDtypeStruct((TABLE, 24, 128), jnp.bfloat16),
-            jax.ShapeDtypeStruct((TILES, 16, 128), jnp.bfloat16),
-        ),
-        in_specs=[anyspace, anyspace],
-        out_specs=(anyspace, anyspace),
-        scratch_shapes=[dma((68,)), dma((32 + SLOTS,)), dma((8,)), dma((TILES,)), dma((16,))],
-        compiler_params=pltpu.CompilerParams(collective_id=0, has_side_effects=True),
-    )(mine, cots)
-
-
-def partial_route(r, c, slot):
-    own = slot < 32
-    main = slot < 64
-    n = slot - 64
-    e = jnp.where(main, slot % 32, jnp.where(n < 2, 2 * c + n, 14 + n))
-    block = jnp.where(own, r, jnp.where(main, r + c, r + 8) % 16)
-    j = 2 * block + e // 16
-    source = jnp.where(own, c, jnp.where(main, 8 + c, 16))
-    return e % 16, j % 8, j // 8, source
+                row = jnp.where(straight, r, (r + 8) & 15)
+                for i in range(COLS if h == 0 else 1):
+                    d = (c + i) & 7 if h == 0 else 0
+                    away = jnp.logical_not(straight) if i == 0 else None
+                    if h == 1:
+                        away = jnp.logical_or(away, c != 0)
+                    op(None, away, row, d, src, tiles.at[4 + h], far_send.at[h * 8 + i], cot_recv.at[4 + h])
+
+
+def partial_routes(r, c):
+    for side, block in ((0, r), (1, (r + c) & 15)):
+        for half in range(2):
+            j = 2 * block + half
+            for i in range(ROWS):
+                t = (r + i) & 15
+                away = (j & 7) != c if i == 0 else None
+                yield None, 32 * side + 16 * half + t, t, j & 7, j >> 3, 8 * side + c, away, 32 * side + 16 * half + i
+    j = 2 * ((r + 8) & 15)
+    for n in range(2):
+        t = 2 * c + n
+        away = jnp.logical_or(t != r, (j & 7) != c)
+        yield None, 64 + n, t, j & 7, j >> 3, 16, away, 64 + n
+    j = j + 1
+    for i in range(ROWS):
+        t = (r + i) & 15
+        away = (j & 7) != c if i == 0 else None
+        yield c == 0, 66 + t, t, j & 7, j >> 3, 16, away, 66 + i
 
 
 def tile_route(r, c, slot):
     far = slot >= 4
     bb, qa = slot // 2, slot % 2
-    other = jnp.where(far, (r + 8) % 16, (r + c) % 16)
-    bb = jnp.where(far, jnp.where(r < 8, qa, 1 - qa), bb)
+    other = (r + 8) & 15 if far else (r + c) & 15
+    if far:
+        bb = jnp.where(r < 8, qa, 1 - qa)
     ahead = other >= r
     i = jnp.where(ahead, 2 * r + bb, 2 * other + qa)
     j = jnp.where(ahead, 2 * other + qa, 2 * r + bb)
-    return i // 2, j % 8, i % 2, j // 8
-
-
-def reduce_kernel(grads, kouts, image_out, kernel_out, parts, far, part_send, part_recv, tile_send, tile_recv, far_recv):
+    return i >> 1, j & 7, i & 1, j >> 3
+
+
+def whole_kernel(mine, cots, image_out, kernel_out, *rest):
+    table, tiles, grads, kouts, parts, far = rest[:6]
+    img_send, img_recv, cot_send, cot_recv, far_send = rest[6:11]
+    part_send, part_recv, tile_send, tile_recv, far_recv = rest[11:16]
     r, c = place()
     enter(r, c)
 
+    def images(op):
+        for idx, (k, rr, cc, slot, away) in enumerate(image_routes(r, c)):
+            op(None, away, rr, cc, mine.at[k], table.at[slot], img_send.at[idx], img_recv.at[slot])
+
+    images(ship)
+    tangents(ship, r, c, cots, tiles, cot_send, cot_recv, far_send)
+    for slot in range(66):
+        arrived(table.at[slot], img_recv.at[slot])
+    for slot in (0, 1, 3, 4):
+        arrived(tiles.at[slot], cot_recv.at[slot])
+
+    @pl.when(c != 0)
+    def _():
+        arrived(tiles.at[2], cot_recv.at[2])
+        for slot in range(66, TABLE):
+            table[slot] = jnp.zeros((24, 128), jnp.bfloat16)
+        tiles[5] = jnp.zeros((16, 128), jnp.bfloat16)
+
+    @pl.when(c == 0)
+    def _():
+        arrived(tiles.at[5], cot_recv.at[5])
+        for slot in range(66, 32 + SLOTS):
+            arrived(table.at[slot], img_recv.at[slot])
+        for slot in range(32 + SLOTS, TABLE):
+            table[slot] = jnp.zeros((24, 128), jnp.bfloat16)
+        tiles[2] = jnp.zeros((16, 128), jnp.bfloat16)
+
+    images(shipped)
+    tangents(shipped, r, c, cots, tiles, cot_send, cot_recv, far_send)
+
+    compute_kernel(32, plan, table, tiles, kouts, grads, *rest[16:])
+
     def partials(op):
-        def step(slot, carry):
-            rr, cc, k, source = partial_route(r, c, slot)
-            op(r, c, rr, cc, grads.at[slot], parts.at[k, source], part_send.at[slot], part_recv.at[k, source])
-            return carry
-
-        lax.fori_loop(0, 32 + slot_count_of(c), step, 0)
+        for go, slot, rr, cc, k, source, away, sem in partial_routes(r, c):
+            op(go, away, rr, cc, grads.at[slot], parts.at[k, source], part_send.at[sem], part_recv.at[k, source])
 
     def outputs(op):
         for slot in range(TILES):
-            rr, cc, h, k = tile_route(r, c, jnp.int32(slot))
-            needed = (None, None, c != 0, None, None, c == 0)[slot]
+            rr, cc, h, k = tile_route(r, c, slot)
+            go = (None, None, c != 0, None, None, c == 0)[slot]
             if slot == 4:
                 dst, sem = far.at[c], far_recv.at[c]
             else:
                 dst, sem = kernel_out.at[h * 4 + k], tile_recv.at[h * 4 + k]
-            if needed is None:
-                op(r, c, rr, cc, kouts.at[slot], dst, tile_send.at[slot], sem)
-            else:
-
-                @pl.when(needed)
-                def _():
-                    op(r, c, rr, cc, kouts.at[slot], dst, tile_send.at[slot], sem)
-
-    partials(send)
-    outputs(send)
+            away = jnp.logical_or(rr != r, cc != c)
+            op(go, away, rr, cc, kouts.at[slot], dst, tile_send.at[slot], sem)
+
+    partials(ship)
+    outputs(ship)
 
     for h in range(2):
         for k in range(4):
             dd, single, straight, rr, cc, slot = cot_route(r, c, h, k)
-            place_ = h * 4 + k
+            spot = h * 4 + k
             if h == 0:
 
                 @pl.when(dd == 8)
@@ -504,7 +467,7 @@
                     total = far[0]
                     for d in range(1, COLS):
                         total = total + far[d]
-                    kernel_out[place_] = total
+                    kernel_out[spot] = total
 
                 get = single
             else:
@@ -512,33 +475,35 @@
 
             @pl.when(get)
             def _():
-                arrived(kernel_out.at[place_], tile_recv.at[place_])
-
-            @pl.when(jnp.logical_or(dd < 0, jnp.logical_and(dd == 0, h > c % 2)))
+                arrived(kernel_out.at[spot], tile_recv.at[spot])
+
+            unused = dd < 0
+            if h == 1:
+                unused = jnp.logical_or(unused, jnp.logical_and(dd == 0, (c & 1) == 0))
+
+            @pl.when(unused)
             def _():
-                kernel_out[place_] = jnp.zeros((16, 128), jnp.float32)
+                kernel_out[spot] = jnp.zeros((16, 128), jnp.float32)
 
     for k in range(4):
-
-        def landed(source, carry):
+        for source in range(17):
             arrived(parts.at[k, source], part_recv.at[k, source])
-            return carry
-
-        lax.fori_loop(0, 17, landed, 0)
         total = parts[k, 0]
         for source in range(1, 17):
             total = total + parts[k, source]
         image_out[k] = total
 
-    partials(sent)
-    outputs(sent)
-
-
-def reduce_call(grads, kouts):
+    partials(shipped)
+    outputs(shipped)
+
+
+def whole_call(mine, cots):
     whole = pl.BlockSpec(memory_space=pltpu.VMEM)
     dma = pltpu.SemaphoreType.DMA
+    vm = lambda *shape: pltpu.VMEM(shape, jnp.float32)
+    own, rows = 32, TABLE * 8
     return pl.pallas_call(
-        reduce_kernel,
+        whole_kernel,
         out_shape=(
             jax.ShapeDtypeStruct((4, 24, 128), jnp.float32),
             jax.ShapeDtypeStruct((8, 16, 128), jnp.float32),
@@ -546,16 +511,24 @@
         in_specs=[whole, whole],
         out_specs=(whole, whole),
         scratch_shapes=[
-            pltpu.VMEM((4, 17, 24, 128), jnp.float32),
-            pltpu.VMEM((8, 16, 128), jnp.float32),
-            dma((32 + SLOTS,)),
-            dma((4, 17)),
-            dma((TILES,)),
-            dma((8,)),
-            dma((8,)),
-        ],
-        compiler_params=pltpu.CompilerParams(collective_id=1, has_side_effects=True),
-    )(grads, kouts)
+            pltpu.VMEM((TABLE, 24, 128), jnp.bfloat16),
+            pltpu.VMEM((TILES, 16, 128), jnp.bfloat16),
+            vm(TABLE, 24, 128),
+            vm(TILES, 16, 128),
+            vm(4, 17, 24, 128),
+            vm(8, 16, 128),
+        ]
+        + [dma((68,)), dma((32 + SLOTS,)), dma((8,)), dma((TILES,)), dma((16,))]
+        + [dma((32 + SLOTS,)), dma((4, 17)), dma((TILES,)), dma((8,)), dma((8,))]
+        + [vm(3, rows, 128)] * 3
+        + [vm(3, 8, own, 128)] * 3
+        + [vm(8, own, 128)] * 6
+        + [vm(rows, 128)] * 6
+        + ([vm(8, 16, 128)] * 5 + [vm(64, 128)] * 6) * 2,
+        compiler_params=pltpu.CompilerParams(
+            collective_id=0, has_side_effects=True, vmem_limit_bytes=56 * 1024 * 1024
+        ),
+    )(mine, cots)
 
 
 def plan():
@@ -583,9 +556,7 @@
     cot = cotangent.reshape(2, 16, 4, 16).transpose(0, 2, 1, 3).reshape(8, 16, 16)
     cots = jnp.concatenate([cot, cot.swapaxes(1, 2)])
     cots = jnp.pad(cots, ((0, 0), (0, 0), (0, 112)))
-    table, tiles = gather_call(mine, cots)
-    kouts, grads = compute_call(32, TILES, plan, table, tiles)
-    image_out, kernel_out = reduce_call(grads, kouts)
+    image_out, kernel_out = whole_call(mine, cots)
     out = kernel_out[:, :, :16].reshape(2, 4, 16, 16)
     half = jnp.arange(2)[:, None, None, None]
     k = jnp.arange(4)[None, :, None, None]

time: 112 us -> 95.1 us (0.85)
  Pallas kernels: 98.6 us -> 81.5 us
    pallas_call x3 -> x1, Pallas kernels: 98.6 us -> 81.5 us  [whole_call(): pl.pallas_call(whole_kernel, out_shape=(jax.ShapeDtypeStruct((4, 24, 128)...]
where the time goes in v3:
time: 95.1 us; the launch traced here: 94.2 us
  Pallas kernels  81.5 us (86%)
  local copies, waits for them, and re-layouts  9.7 us (10%)
  other arithmetic  2.3 us (2%)
    pallas_call x1, Pallas kernels, whole_call(): pl.pallas_call(whole_kernel, out_shape=(jax.ShapeDtypeStruct((4, 24, 128)...  81.5 us
    reshape x2, local copies, waits for them, and re-layouts, from_rows(): rows.reshape(count, 3, 4, 2, 8, 16).transpose(0, 1, 4, 2, 5, 3)  2.39 us
    unnamed x2, local copies, waits for them, and re-layouts  2.25 us

profile of v3, /device:TPU:1, one launch (start us, length us, event | category | flops | bytes accessed | tf_op | source)
XLA Modules:
  0.0 94.2 jit_solution(17870847521836284828)
XLA Ops:
  0.7 0.1 and_or_fusion
  0.8 0.8 copy.18
  1.5 0.8 copy.12
  2.4 0.7 fusion.2.cots
  3.0 1.2 %copy.10 = bf16[4,1,1,3072]{0,3,2,1:T(8,128)(2,1)S(1)} copy(bf16[4,1,1,3072]{3,0,2,1:T(4,128)(2,1)} %param.2) | data formatting | bytes 49152 | tf_op args[0]
  4.2 1.8 %copy.11 = bf16[4,3,4,2,8,16]{5,4,3,2,1,0:T(8,128)(2,1)S(1)} copy(bf16[4,3,4,2,8,16]{0,3,5,2,4,1:T(2,128)(2,1)S(1)} %bitcast.23) | data formatting | bytes 49152 | tf_op jit(solution)/shard_map/transpose | solution.py:252
  6.0 0.8 reshape.89.mine
  6.7 81.5 %shard_map.41 = (f32[4,24,128]{2,1,0:T(8,128)}, f32[8,16,128]{2,1,0:T(8,128)}) custom-call(bf16[4,24,128]{2,1,0:T(8,128)(2,1)} %reshape.89.mine, bf16[16,16,128]{2,1,0:T(8,128)(2,1)} %fusion.2.cots), custom_call_target="tpu_custom_call" | custom-call | tf_op jit(solution)/shard_map/pallas_call | solution.py:505
  88.2 0.9 copy.14
  89.1 1.6 %bitcast_select_fusion = f32[2,4,16,16]{3,1,2,0:T(4,128)} fusion(f32[2,4,16,16]{2,1,3,0:T(4,128)S(1)} %copy.14, f32[2,4,16,16]{3,2,1,0:T(8,128)} %bitcast.25, pred[2,4]{1,0:T(4,128)(4,1)S(1)} %and_or_fusion), kind=kLoop, calls=%fused_computation.4 | loop fusion | flops 2048 | bytes 24584 | tf_op jit(solution)/shard_map/jit(_where)/select_n | solution.py:565
  90.7 0.9 %reshape.94 = f32[4,3,4,2,8,16]{5,4,3,2,1,0:T(8,128)S(1)} reshape(f32[4,24,128]{2,1,0:T(8,128)} %get-tuple-element.5) | data formatting | bytes 98304 | tf_op jit(solution)/shard_map/reshape | solution.py:257
  91.6 1.4 %copy.16 = f32[4,3,4,2,8,16]{0,3,5,2,4,1:T(2,128)S(1)} copy(f32[4,3,4,2,8,16]{5,4,3,2,1,0:T(8,128)S(1)} %reshape.94) | data formatting | bytes 98304 | tf_op jit(solution)/shard_map/reshape | solution.py:257
  93.1 1.1 %copy.17 = f32[4,1,1,3072]{3,2,1,0:T(1,128)} copy(f32[4,1,1,3072]{0,3,2,1:T(8,128)S(1)} %bitcast.22) | data formatting | bytes 98304
  (2 shorter events, 0.0 us)

commit v4 on v3

--- a/solution.py
+++ b/solution.py
@@ -40,7 +40,7 @@
     )
 
 
-def compute_kernel(n_own, plan, img, cot, kout, grad, xa, ra, ta, xb, rb, tb, *rest):
+def compute_kernel(n_own, plan, landed, finished, img, cot, kout, grad, xa, ra, ta, xb, rb, tb, *rest):
     ub, ua, save = rest[:6], rest[6:12], (rest[12:23], rest[23:34])
     f32 = jnp.float32
     unit_count, slot_count, unit_of = plan()
@@ -82,8 +82,18 @@
             ua[k][at8, :] = jnp.zeros((BATCH * 8, 128), f32)
         return carry
 
-    batches = (n_own + slot_count + BATCH - 1) // BATCH
-    lax.fori_loop(0, batches, prologue, 0)
+    more = slot_count > 34
+
+    def fetched(step, carry):
+        landed(step)
+        return prologue(step, carry)
+
+    lax.fori_loop(0, 9, fetched, 0)
+
+    @pl.when(more)
+    def _():
+        lax.fori_loop(9, TABLE // BATCH, fetched, 0)
+
 
     for group in range(n_own // 8):
         for s in range(8):
@@ -125,11 +135,10 @@
     ORDER = (0, 7, 1, 6, 2, 5, 3, 4)
 
     def ready(u):
-        live = u < unit_count
-        slot, bb, tile, lane = unit_of(jnp.minimum(u, unit_count - 1))
+        slot, bb, tile, lane = unit_of(u)
         base = pl.multiple_of((n_own + slot) * 8, 8)
         own = pl.ds(pl.multiple_of(bb * 16, 16), 16)
-        return live, base, own, tile, lane
+        return base, own, tile, lane
 
     def arow(ref, q, base, s):
         return ref[q, pl.ds(base + s, 1), :]
@@ -146,7 +155,7 @@
 
     def forward(u, saved):
         sg1, sz1, sg2, sz2, sh, *uacc = saved
-        live, base, own, tile, lane = ready(u)
+        base, own, tile, lane = ready(u)
         h = [None] * 8
         for s in ORDER:
             x = xb[0, s, own, :] * arow(xa, 0, base, s)
@@ -156,7 +165,7 @@
         h = across(h)
         weight = jnp.where(lane16 == lane, cot[tile].astype(f32), 0.0)
         weight = jnp.sum(weight, axis=1, keepdims=True) * (WEIGHT_VAR * ALPHA[2] / 1024.0)
-        weight = jnp.where(live, jnp.broadcast_to(weight, (16, 128)), 0.0)
+        weight = jnp.broadcast_to(weight, (16, 128))
         total = None
         for layer in range(LAYERS):
             w = vertical(h, BIAS[layer])
@@ -190,7 +199,7 @@
 
     def backward(u, saved):
         sg1, sz1, sg2, sz2, sh, *uacc = saved
-        live, base, own, tile, lane = ready(u)
+        base, own, tile, lane = ready(u)
         h = [sh[s] for s in range(8)]
         for layer in range(LAYERS - 2, -1, -1):
             w = vertical(h, None)
@@ -217,14 +226,6 @@
         backward(2 * i + 1, save[1])
         forward(2 * i + 3, save[1])
         return carry
-
-    lax.fori_loop(0, unit_count // 2, pair, 0)
-
-    for group in range(n_own // 8):
-        for s in range(8):
-            rows = pl.ds(group * 64 + s, 8, stride=8)
-            for k in range(6):
-                ua[k][rows, :] = ub[k][s, group * 8 : group * 8 + 8, :]
 
     def epilogue(step, carry):
         at = pl.multiple_of(step * BATCH, BATCH)
@@ -244,7 +245,33 @@
             grad[pl.ds(at, BATCH), q * 8 : q * 8 + 8, :] = part + down * x
         return carry
 
-    lax.fori_loop(0, batches, epilogue, 0)
+    def segment(n, carry):
+        lax.fori_loop(8 * n, 8 * n + 8, pair, 0)
+        epilogue(4 + n, 0)
+        finished(4 + n)
+        return carry
+
+    lax.fori_loop(0, 4, segment, 0)
+    backward(jnp.int32(unit_count - 2), save[0])
+    backward(jnp.int32(unit_count - 1), save[1])
+
+    for group in range(n_own // 8):
+        for s in range(8):
+            rows = pl.ds(group * 64 + s, 8, stride=8)
+            for k in range(6):
+                ua[k][rows, :] = ub[k][s, group * 8 : group * 8 + 8, :]
+
+    def last(step, carry):
+        epilogue(step, 0)
+        finished(step)
+        return carry
+
+    lax.fori_loop(0, 4, last, 0)
+    last(8, 0)
+
+    @pl.when(more)
+    def _():
+        lax.fori_loop(9, TABLE // BATCH, last, 0)
 
 
 def to_rows(images):
@@ -270,13 +297,22 @@
     return lax.axis_index("row"), lax.axis_index("col")
 
 
-def enter(r, c):
+def greet(r, c):
     barrier = pltpu.get_barrier_semaphore()
-    me = r * COLS + c
-    for i in range(1, ROWS * COLS):
-        peer = (me + i) & (ROWS * COLS - 1)
-        pl.semaphore_signal(barrier, inc=1, device_id=(peer >> 3, peer & 7), device_id_type=MESH)
-    pl.semaphore_wait(barrier, ROWS * COLS - 1)
+    x, y, z = (r >> 1) & 3, c >> 1, ((c & 1) << 1) + (r >> 3)
+    xs = [((x + d) & 3) << 1 for d in range(4)]
+    ys = [((y + d) & 3) << 1 for d in range(4)]
+    zs = [((z + d) & 3) for d in range(4)]
+    cores = [r & 1, 1 - (r & 1)]
+    far = lambda o: sum(min(d, 4 - d) for d in o[:3]) + 0.1 * o[3]
+    steps = [(i, j, k, l) for i in range(4) for j in range(4) for k in range(4) for l in range(2)]
+    for i, j, k, l in sorted(steps, key=far, reverse=True)[:-1]:
+        rr = ((zs[k] & 1) << 3) + xs[i] + cores[l]
+        pl.semaphore_signal(barrier, inc=1, device_id=(rr, ys[j] + (zs[k] >> 1)), device_id_type=MESH)
+
+
+def enter():
+    pl.semaphore_wait(pltpu.get_barrier_semaphore(), ROWS * COLS - 1)
 
 
 def ship(go, away, rr, cc, src, dst, send_sem, recv_sem):
@@ -365,24 +401,16 @@
                     op(None, away, row, d, src, tiles.at[4 + h], far_send.at[h * 8 + i], cot_recv.at[4 + h])
 
 
-def partial_routes(r, c):
-    for side, block in ((0, r), (1, (r + c) & 15)):
-        for half in range(2):
-            j = 2 * block + half
-            for i in range(ROWS):
-                t = (r + i) & 15
-                away = (j & 7) != c if i == 0 else None
-                yield None, 32 * side + 16 * half + t, t, j & 7, j >> 3, 8 * side + c, away, 32 * side + 16 * half + i
-    j = 2 * ((r + 8) & 15)
-    for n in range(2):
-        t = 2 * c + n
-        away = jnp.logical_or(t != r, (j & 7) != c)
-        yield None, 64 + n, t, j & 7, j >> 3, 16, away, 64 + n
-    j = j + 1
-    for i in range(ROWS):
-        t = (r + i) & 15
-        away = (j & 7) != c if i == 0 else None
-        yield c == 0, 66 + t, t, j & 7, j >> 3, 16, away, 66 + i
+def partial_route(r, c, batch, n):
+    slot = batch * BATCH + n
+    main = batch < 8
+    own = batch < 4
+    x = slot - 64
+    e = jnp.where(main, slot & 31, jnp.where(x < 2, 2 * c + x, 14 + x))
+    block = jnp.where(own, r, jnp.where(main, r + c, r + 8) & 15)
+    j = 2 * block + (e >> 4)
+    source = jnp.where(own, c, jnp.where(main, 8 + c, 16))
+    return slot, e & 15, j & 7, j >> 3, source
 
 
 def tile_route(r, c, slot):
@@ -402,7 +430,8 @@
     img_send, img_recv, cot_send, cot_recv, far_send = rest[6:11]
     part_send, part_recv, tile_send, tile_recv, far_recv = rest[11:16]
     r, c = place()
-    enter(r, c)
+    greet(r, c)
+    enter()
 
     def images(op):
         for idx, (k, rr, cc, slot, away) in enumerate(image_routes(r, c)):
@@ -410,35 +439,41 @@
 
     images(ship)
     tangents(ship, r, c, cots, tiles, cot_send, cot_recv, far_send)
-    for slot in range(66):
-        arrived(table.at[slot], img_recv.at[slot])
     for slot in (0, 1, 3, 4):
         arrived(tiles.at[slot], cot_recv.at[slot])
 
     @pl.when(c != 0)
     def _():
         arrived(tiles.at[2], cot_recv.at[2])
-        for slot in range(66, TABLE):
+        tiles[5] = jnp.zeros((16, 128), jnp.bfloat16)
+        for slot in range(66, 72):
             table[slot] = jnp.zeros((24, 128), jnp.bfloat16)
-        tiles[5] = jnp.zeros((16, 128), jnp.bfloat16)
 
     @pl.when(c == 0)
     def _():
         arrived(tiles.at[5], cot_recv.at[5])
-        for slot in range(66, 32 + SLOTS):
-            arrived(table.at[slot], img_recv.at[slot])
+        tiles[2] = jnp.zeros((16, 128), jnp.bfloat16)
         for slot in range(32 + SLOTS, TABLE):
             table[slot] = jnp.zeros((24, 128), jnp.bfloat16)
-        tiles[2] = jnp.zeros((16, 128), jnp.bfloat16)
-
-    images(shipped)
-    tangents(shipped, r, c, cots, tiles, cot_send, cot_recv, far_send)
-
-    compute_kernel(32, plan, table, tiles, kouts, grads, *rest[16:])
-
-    def partials(op):
-        for go, slot, rr, cc, k, source, away, sem in partial_routes(r, c):
-            op(go, away, rr, cc, grads.at[slot], parts.at[k, source], part_send.at[sem], part_recv.at[k, source])
+
+    def used(batch, n):
+        slot = batch * BATCH + n
+        return jnp.logical_or(slot < 66, jnp.logical_and(c == 0, slot < 32 + SLOTS))
+
+    def landed(batch):
+        for n in range(BATCH):
+            slot = batch * BATCH + n
+            guarded(used(batch, n), None, lambda: arrived(table.at[slot], img_recv.at[slot]))
+
+    def partials(op, batch):
+        for n in range(BATCH):
+            slot, rr, cc, k, source = partial_route(r, c, batch, n)
+            away = jnp.logical_or(rr != r, cc != c)
+            op(used(batch, n), away, rr, cc, grads.at[slot], parts.at[k, source], part_send.at[slot], part_recv.at[k, source])
+
+    compute_kernel(
+        32, plan, landed, lambda batch: partials(ship, batch), table, tiles, kouts, grads, *rest[16:]
+    )
 
     def outputs(op):
         for slot in range(TILES):
@@ -451,7 +486,6 @@
             away = jnp.logical_or(rr != r, cc != c)
             op(go, away, rr, cc, kouts.at[slot], dst, tile_send.at[slot], sem)
 
-    partials(ship)
     outputs(ship)
 
     for h in range(2):
@@ -493,8 +527,15 @@
             total = total + parts[k, source]
         image_out[k] = total
 
-    partials(shipped)
+    images(shipped)
+    tangents(shipped, r, c, cots, tiles, cot_send, cot_recv, far_send)
     outputs(shipped)
+
+    def settle(batch, carry):
+        partials(shipped, batch)
+        return carry
+
+    lax.fori_loop(0, TABLE // BATCH, settle, 0)
 
 
 def whole_call(mine, cots):

time: 95.1 us -> 88.1 us (0.926)
  Pallas kernels: 81.5 us -> 74.9 us
    pallas_call x1, Pallas kernels: 81.5 us -> 74.9 us  [whole_call(): pl.pallas_call(whole_kernel, out_shape=(jax.ShapeDtypeStruct((4, 24, 128)...]
where the time goes in v4:
time: 88.1 us; the launch traced here: 87.6 us
  Pallas kernels  74.9 us (85%)
  local copies, waits for them, and re-layouts  9.7 us (11%)
  other arithmetic  2.3 us (3%)
    pallas_call x1, Pallas kernels, whole_call(): pl.pallas_call(whole_kernel, out_shape=(jax.ShapeDtypeStruct((4, 24, 128)...  74.9 us
    reshape x2, local copies, waits for them, and re-layouts, from_rows(): rows.reshape(count, 3, 4, 2, 8, 16).transpose(0, 1, 4, 2, 5, 3)  2.39 us
    unnamed x2, local copies, waits for them, and re-layouts  2.25 us

profile of v4, /device:TPU:1, one launch (start us, length us, event | category | flops | bytes accessed | tf_op | source)
XLA Modules:
  0.0 87.6 jit_solution(12358395344930304170)
XLA Ops:
  0.7 0.1 and_or_fusion
  0.8 0.8 copy.18
  1.5 0.8 copy.12
  2.4 0.7 fusion.2.cots
  3.0 1.2 %copy.10 = bf16[4,1,1,3072]{0,3,2,1:T(8,128)(2,1)S(1)} copy(bf16[4,1,1,3072]{3,0,2,1:T(4,128)(2,1)} %param.2) | data formatting | bytes 49152 | tf_op args[0]
  4.2 1.8 %copy.11 = bf16[4,3,4,2,8,16]{5,4,3,2,1,0:T(8,128)(2,1)S(1)} copy(bf16[4,3,4,2,8,16]{0,3,5,2,4,1:T(2,128)(2,1)S(1)} %bitcast.23) | data formatting | bytes 49152 | tf_op jit(solution)/shard_map/transpose | solution.py:279
  6.0 0.8 reshape.89.mine
  6.7 74.9 %shard_map.41 = (f32[4,24,128]{2,1,0:T(8,128)}, f32[8,16,128]{2,1,0:T(8,128)}) custom-call(bf16[4,24,128]{2,1,0:T(8,128)(2,1)} %reshape.89.mine, bf16[16,16,128]{2,1,0:T(8,128)(2,1)} %fusion.2.cots), custom_call_target="tpu_custom_call" | custom-call | tf_op jit(solution)/shard_map/pallas_call | solution.py:546
  81.6 0.9 %copy.14 = f32[2,4,16,16]{2,1,3,0:T(4,128)S(1)} copy(f32[2,4,16,16]{3,2,1,0:T(8,128)} %bitcast.24) | data formatting | bytes 16384 | tf_op jit(solution)/shard_map/reshape | solution.py:601
  82.6 1.6 %bitcast_select_fusion = f32[2,4,16,16]{3,1,2,0:T(4,128)} fusion(f32[2,4,16,16]{2,1,3,0:T(4,128)S(1)} %copy.14, f32[2,4,16,16]{3,2,1,0:T(8,128)} %bitcast.25, pred[2,4]{1,0:T(4,128)(4,1)S(1)} %and_or_fusion), kind=kLoop, calls=%fused_computation.4 | loop fusion | flops 2048 | bytes 24584 | tf_op jit(solution)/shard_map/jit(_where)/select_n | solution.py:606
  84.1 0.9 %reshape.94 = f32[4,3,4,2,8,16]{5,4,3,2,1,0:T(8,128)S(1)} reshape(f32[4,24,128]{2,1,0:T(8,128)} %get-tuple-element.5) | data formatting | bytes 98304 | tf_op jit(solution)/shard_map/reshape | solution.py:284
  85.1 1.4 %copy.16 = f32[4,3,4,2,8,16]{0,3,5,2,4,1:T(2,128)S(1)} copy(f32[4,3,4,2,8,16]{5,4,3,2,1,0:T(8,128)S(1)} %reshape.94) | data formatting | bytes 98304 | tf_op jit(solution)/shard_map/reshape | solution.py:284
  86.5 1.1 %copy.17 = f32[4,1,1,3072]{3,2,1,0:T(1,128)} copy(f32[4,1,1,3072]{0,3,2,1:T(8,128)S(1)} %bitcast.22) | data formatting | bytes 98304
  (2 shorter events, 0.0 us)

commit v5 on v4

--- a/solution.py
+++ b/solution.py
@@ -43,7 +43,7 @@
 def compute_kernel(n_own, plan, landed, finished, img, cot, kout, grad, xa, ra, ta, xb, rb, tb, *rest):
     ub, ua, save = rest[:6], rest[6:12], (rest[12:23], rest[23:34])
     f32 = jnp.float32
-    unit_count, slot_count, unit_of = plan()
+    unit_count, slot_count, unit_of, turned = plan()
     left, right, upper, lower = lane_masks((16, 128))
 
     row3 = lax.broadcasted_iota(jnp.int32, (BATCH, 8, 128), 1)
@@ -132,6 +132,7 @@
         return w
 
     lane16 = lax.broadcasted_iota(jnp.int32, (16, 128), 1)
+    row16 = lax.broadcasted_iota(jnp.int32, (16, 128), 0)
     ORDER = (0, 7, 1, 6, 2, 5, 3, 4)
 
     def ready(u):
@@ -163,7 +164,10 @@
             x = x + xb[2, s, own, :] * arow(xa, 2, base, s)
             h[s] = x
         h = across(h)
-        weight = jnp.where(lane16 == lane, cot[tile].astype(f32), 0.0)
+        spin = turned(u)
+        row = cot[pl.ds(tile * 16 + lane, 1), :]
+        source = jnp.where(spin, jnp.broadcast_to(row, (16, 128)), cot[pl.ds(pl.multiple_of(tile * 16, 16), 16), :])
+        weight = jnp.where(lane16 == jnp.where(spin, row16, lane), source, 0.0)
         weight = jnp.sum(weight, axis=1, keepdims=True) * (WEIGHT_VAR * ALPHA[2] / 1024.0)
         weight = jnp.broadcast_to(weight, (16, 128))
         total = None
@@ -195,7 +199,10 @@
             sh[s] = h[s]
         fold(uacc, LAYERS - 1, base)
         value = jnp.sum(total, axis=1, keepdims=True) * (WEIGHT_VAR * ALPHA[2] / 1024.0) + BIAS_VAR
-        kout[tile] = jnp.where(lane16 == lane, value, kout[tile])
+        value = jnp.broadcast_to(value, (16, 128))
+        flat = jnp.sum(jnp.where(lane16 == row16, value, 0.0), axis=0, keepdims=True)
+        value = jnp.where(spin, jnp.broadcast_to(flat, (16, 128)), value)
+        kout[tile] = jnp.where(jnp.where(spin, row16, lane16) == lane, value, kout[tile])
 
     def backward(u, saved):
         sg1, sz1, sg2, sz2, sh, *uacc = saved
@@ -274,14 +281,48 @@
         lax.fori_loop(9, TABLE // BATCH, last, 0)
 
 
-def to_rows(images):
-    count = images.shape[0]
-    return images.reshape(count, 3, 8, 4, 16, 2).transpose(0, 1, 3, 5, 2, 4).reshape(count, 24, 128)
-
-
-def from_rows(rows):
-    count = rows.shape[0]
-    return rows.reshape(count, 3, 4, 2, 8, 16).transpose(0, 1, 4, 2, 5, 3).reshape(count, 3072)
+def lane_order(flip):
+    a = lax.broadcasted_iota(jnp.int32, (128, 128), 1 if flip else 0)
+    b = lax.broadcasted_iota(jnp.int32, (128, 128), 0 if flip else 1)
+    to = ((a >> 5) * 2 + (a & 1)) * 16 + ((a >> 1) & 15)
+    return jnp.where(to == b, 1.0, 0.0)
+
+
+def swap_groups(rows):
+    group = lax.broadcasted_iota(jnp.int32, rows[0].shape, 1) >> 4
+    out = []
+    for s in range(8):
+        total = rows[s]
+        for j in range(8):
+            if j != s:
+                total = jnp.where(group == j, pltpu.roll(rows[j], (j - s) * 16 % 128, 1), total)
+        out.append(total)
+    return out
+
+
+def to_rows(images, spread, mine):
+    order = lane_order(False).astype(jnp.bfloat16)
+    for ch in range(3):
+        tall = jnp.concatenate(
+            [images[:, (ch * 8 + j) * 128 : (ch * 8 + j + 1) * 128].astype(jnp.float32) for j in range(8)]
+        )
+        tall = jnp.dot(tall.astype(jnp.bfloat16), order, preferred_element_type=jnp.float32)
+        rows = swap_groups([tall[4 * j : 4 * j + 4] for j in range(8)])
+        for s in range(8):
+            spread[pl.ds(ch * 8 + s, 4, stride=24), :] = rows[s]
+    for k in range(4):
+        mine[k] = spread[24 * k : 24 * k + 24, :].astype(jnp.bfloat16)
+
+
+def from_rows(spread, out):
+    order = lane_order(True)
+    for ch in range(3):
+        rows = swap_groups([spread[pl.ds(ch * 8 + s, 4, stride=24), :] for s in range(8)])
+        tall = jnp.dot(
+            jnp.concatenate(rows), order, precision=lax.Precision.HIGHEST, preferred_element_type=jnp.float32
+        )
+        for j in range(8):
+            out[:, (ch * 8 + j) * 128 : (ch * 8 + j + 1) * 128] = tall[4 * j : 4 * j + 4]
 
 
 ROWS = 16
@@ -387,7 +428,7 @@
         for k in range(4):
             idx = h * 4 + k
             dd, single, straight, rr, cc, slot = cot_route(r, c, h, k)
-            src = cots.at[jnp.where(straight, idx, 8 + idx)]
+            src = cots.at[idx]
             op(single, dd != c, rr, cc, src, tiles.at[slot], cot_send.at[idx], cot_recv.at[slot])
 
             @pl.when(dd == 8)
@@ -425,12 +466,20 @@
     return i >> 1, j & 7, i & 1, j >> 3
 
 
-def whole_kernel(mine, cots, image_out, kernel_out, *rest):
+def whole_kernel(images_in, cot_in, images_out, kernel_ref, mine, cots, spread, cot32, kernel_out, *rest):
     table, tiles, grads, kouts, parts, far = rest[:6]
     img_send, img_recv, cot_send, cot_recv, far_send = rest[6:11]
     part_send, part_recv, tile_send, tile_recv, far_recv = rest[11:16]
     r, c = place()
     greet(r, c)
+    to_rows(images_in, spread, mine)
+    cot32[...] = jnp.zeros_like(cot32)
+    for h in range(2):
+        for row in range(16):
+            part = cot_in[h, row].astype(jnp.float32)
+            cot32[pl.ds(h * 64 + row, 4, stride=16), 0:16] = part
+    for idx in range(8):
+        cots[idx] = cot32[16 * idx : 16 * idx + 16, :].astype(jnp.bfloat16)
     enter()
 
     def images(op):
@@ -471,8 +520,11 @@
             away = jnp.logical_or(rr != r, cc != c)
             op(used(batch, n), away, rr, cc, grads.at[slot], parts.at[k, source], part_send.at[slot], part_recv.at[k, source])
 
+    for slot in range(TILES):
+        cot32[16 * slot : 16 * slot + 16, :] = tiles[slot].astype(jnp.float32)
+
     compute_kernel(
-        32, plan, landed, lambda batch: partials(ship, batch), table, tiles, kouts, grads, *rest[16:]
+        32, plan, landed, lambda batch: partials(ship, batch), table, cot32, kouts, grads, *rest[16:]
     )
 
     def outputs(op):
@@ -482,7 +534,7 @@
             if slot == 4:
                 dst, sem = far.at[c], far_recv.at[c]
             else:
-                dst, sem = kernel_out.at[h * 4 + k], tile_recv.at[h * 4 + k]
+                dst, sem = kernel_out.at[pl.ds(pl.multiple_of((h * 4 + k) * 16, 16), 16)], tile_recv.at[h * 4 + k]
             away = jnp.logical_or(rr != r, cc != c)
             op(go, away, rr, cc, kouts.at[slot], dst, tile_send.at[slot], sem)
 
@@ -501,7 +553,7 @@
                     total = far[0]
                     for d in range(1, COLS):
                         total = total + far[d]
-                    kernel_out[spot] = total
+                    kernel_out[16 * spot : 16 * spot + 16, :] = total
 
                 get = single
             else:
@@ -509,7 +561,7 @@
 
             @pl.when(get)
             def _():
-                arrived(kernel_out.at[spot], tile_recv.at[spot])
+                arrived(kernel_out.at[16 * spot : 16 * spot + 16], tile_recv.at[spot])
 
             unused = dd < 0
             if h == 1:
@@ -517,7 +569,7 @@
 
             @pl.when(unused)
             def _():
-                kernel_out[spot] = jnp.zeros((16, 128), jnp.float32)
+                kernel_out[16 * spot : 16 * spot + 16, :] = jnp.zeros((16, 128), jnp.float32)
 
     for k in range(4):
         for source in range(17):
@@ -525,8 +577,12 @@
         total = parts[k, 0]
         for source in range(1, 17):
             total = total + parts[k, source]
-        image_out[k] = total
-
+        spread[24 * k : 24 * k + 24, :] = total
+
+    from_rows(spread, images_out)
+    for h in range(2):
+        for row in range(16):
+            kernel_ref[h, row] = kernel_out[pl.ds(h * 64 + row, 4, stride=16), :][:, 0:16]
     images(shipped)
     tangents(shipped, r, c, cots, tiles, cot_send, cot_recv, far_send)
     outputs(shipped)
@@ -546,12 +602,17 @@
     return pl.pallas_call(
         whole_kernel,
         out_shape=(
-            jax.ShapeDtypeStruct((4, 24, 128), jnp.float32),
-            jax.ShapeDtypeStruct((8, 16, 128), jnp.float32),
+            jax.ShapeDtypeStruct((4, 3072), jnp.float32),
+            jax.ShapeDtypeStruct((2, 16, 4, 16), jnp.float32),
         ),
         in_specs=[whole, whole],
         out_specs=(whole, whole),
         scratch_shapes=[
+            pltpu.VMEM((4, 24, 128), jnp.bfloat16),
+            pltpu.VMEM((8, 16, 128), jnp.bfloat16),
+            vm(96, 128),
+            vm(128, 128),
+            vm(128, 128),
             pltpu.VMEM((TABLE, 24, 128), jnp.bfloat16),
             pltpu.VMEM((TILES, 16, 128), jnp.bfloat16),
             vm(TABLE, 24, 128),
@@ -588,24 +649,15 @@
         tile = jnp.where(main, bb * 2 + slot // 16, 4 + e // 16)
         return slot, bb, tile, jnp.where(main, slot, e) % 16
 
-    return 66, slot_count_of(c), unit_of
+    def turned(u):
+        return jnp.where(u < jnp.where(c == 0, 48, 64), r + c >= ROWS, r >= 8)
+
+    return 66, slot_count_of(c), unit_of, turned
 
 
 def body(images, cotangent):
-    r, c = place()
-    mine = to_rows(images.reshape(4, 3072))
-    cot = cotangent.reshape(2, 16, 4, 16).transpose(0, 2, 1, 3).reshape(8, 16, 16)
-    cots = jnp.concatenate([cot, cot.swapaxes(1, 2)])
-    cots = jnp.pad(cots, ((0, 0), (0, 0), (0, 112)))
-    image_out, kernel_out = whole_call(mine, cots)
-    out = kernel_out[:, :, :16].reshape(2, 4, 16, 16)
-    half = jnp.arange(2)[:, None, None, None]
-    k = jnp.arange(4)[None, :, None, None]
-    dd = 4 * k + c // 2 - r
-    straight = jnp.logical_or(dd < 8, jnp.logical_and(dd == 8, half == c % 2))
-    out = jnp.where(straight, out, out.swapaxes(2, 3))
-    kernel = out.transpose(0, 2, 1, 3).reshape(2, 16, 4, 1, 16)
-    return kernel, from_rows(image_out).reshape(4, 1, 1, 3072)
+    image_grads, kernel = whole_call(images.reshape(4, 3072), cotangent.reshape(2, 16, 4, 16))
+    return kernel.reshape(2, 16, 4, 1, 16), image_grads.reshape(4, 1, 1, 3072)
 
 
 def solution(mesh):

time: 88.1 us -> 78.9 us (0.90)
  local copies, waits for them, and re-layouts: 9.7 us -> 2.13 us
  other arithmetic: 2.3 us -> 0 us
  Pallas kernels: 74.9 us -> 75.9 us
    reshape x5 -> x0, local copies, waits for them, and re-layouts: 4.85 us -> none  [the longest x2 2.39 us: from_rows(): rows.reshape(count, 3, 4, 2, 8, 16).transpose(0, 1, 4, 2, 5, 3)]
    transpose x2 -> x0, local copies, waits for them, and re-layouts: 2.61 us -> none  [the longest x1 1.76 us: to_rows(): images.reshape(count, 3, 8, 4, 16, 2).transpose(0, 1, 3, 5, 2, 4)]
    select_n x1 -> x0, other arithmetic: 1.55 us -> none  [body(): out = jnp.where(straight, out, out.swapaxes(2, 3))]
    pallas_call x1, Pallas kernels: 74.9 us -> 75.9 us  [whole_call(): pl.pallas_call(whole_kernel, out_shape=(jax.ShapeDtypeStruct((4, 3072), j...]
    unnamed x2 -> x4, local copies, waits for them, and re-layouts: 2.25 us -> 2.13 us
where the time goes in v5:
time: 78.9 us; the launch traced here: 78.6 us
  Pallas kernels  75.9 us (96%)
  local copies, waits for them, and re-layouts  2.13 us (3%)
    pallas_call x1, Pallas kernels, whole_call(): pl.pallas_call(whole_kernel, out_shape=(jax.ShapeDtypeStruct((4, 3072), j...  75.9 us
    unnamed x4, local copies, waits for them, and re-layouts  2.13 us

profile of v5, /device:TPU:1, one launch (start us, length us, event | category | flops | bytes accessed | tf_op | source)
XLA Modules:
  0.0 78.6 jit_solution(18171903552781400144)
XLA Ops:
  0.6 75.9 %shard_map.41 = (f32[4,3072]{1,0:T(4,128)}, f32[2,16,4,16]{3,2,1,0:T(4,128)}) custom-call(bf16[4,3072]{1,0:T(4,128)(2,1)} %bitcast.9, bf16[2,16,4,16]{3,2,1,0:T(4,128)(2,1)} %bitcast.8), custom_call_target="tpu_custom_call" | custom-call | tf_op jit(solution)/shard_map/pallas_call | solution.py:602
  76.5 0.0 copy-start
  76.5 1.5 %copy.5 = f32[4,1,1,3072]{3,2,1,0:T(1,128)} copy(f32[4,1,1,3072]{3,0,2,1:T(4,128)} %bitcast.7) | data formatting | bytes 98304
  78.0 0.0 copy-done
  78.0 0.6 copy.7
Async XLA Ops:
  76.5 1.5 %copy-start = (f32[2,16,4,16]{3,2,1,0:T(4,128)S(1)}, f32[2,16,4,16]{3,2,1,0:T(4,128)}, u32[]{:S(2)}) copy-start(f32[2,16,4,16]{3,2,1,0:T(4,128)} %get-tuple-element.4) | copy-start | bytes 24580

commit v6 on v5

--- a/solution.py
+++ b/solution.py
@@ -40,7 +40,7 @@
     )
 
 
-def compute_kernel(n_own, plan, landed, finished, img, cot, kout, grad, xa, ra, ta, xb, rb, tb, *rest):
+def compute_kernel(n_own, plan, landed, finished, tiled, img, cot, kout, grad, xa, ra, ta, xb, rb, tb, *rest):
     ub, ua, save = rest[:6], rest[6:12], (rest[12:23], rest[23:34])
     f32 = jnp.float32
     unit_count, slot_count, unit_of, turned = plan()
@@ -88,12 +88,9 @@
         landed(step)
         return prologue(step, carry)
 
-    lax.fori_loop(0, 9, fetched, 0)
-
-    @pl.when(more)
-    def _():
-        lax.fori_loop(9, TABLE // BATCH, fetched, 0)
-
+    lax.fori_loop(0, 4, fetched, 0)
+    lax.fori_loop(8, jnp.where(more, TABLE // BATCH, 9), fetched, 0)
+    fetched(4, 0)
 
     for group in range(n_own // 8):
         for s in range(8):
@@ -227,11 +224,36 @@
     forward(jnp.int32(0), save[0])
     forward(jnp.int32(1), save[1])
 
-    def pair(i, carry):
-        backward(2 * i, save[0])
-        forward(2 * i + 2, save[0])
-        backward(2 * i + 1, save[1])
-        forward(2 * i + 3, save[1])
+    def gather_own(block):
+        for group in (2 * block, 2 * block + 1):
+            for s in range(8):
+                rows = pl.ds(group * 64 + s, 8, stride=8)
+                for k in range(6):
+                    ua[k][rows, :] = ub[k][s, group * 8 : group * 8 + 8, :]
+
+    def pairs(j, carry):
+        @pl.when(jnp.logical_or(j == 2, jnp.logical_or(j == 4, j == 6)))
+        def _():
+            fetched(4 + (j >> 1), 0)
+
+        for n in range(2):
+            u = 4 * j + 2 * n
+            backward(u, save[0])
+            forward(u + 2, save[0])
+            backward(u + 1, save[1])
+            forward(u + 3, save[1])
+
+        @pl.when(jnp.logical_or(j == 4, jnp.logical_or(j == 10, jnp.logical_or(j == 12, j == 14))))
+        def _():
+            low = jnp.where(j == 4, 8, (j >> 1) - 1)
+            high = jnp.where(jnp.logical_and(j == 4, more), TABLE // BATCH, low + 1)
+            lax.fori_loop(low, high, last, 0)
+
+        @pl.when(j == 12)
+        def _():
+            gather_own(0)
+            lax.fori_loop(0, 2, last, 0)
+
         return carry
 
     def epilogue(step, carry):
@@ -252,33 +274,18 @@
             grad[pl.ds(at, BATCH), q * 8 : q * 8 + 8, :] = part + down * x
         return carry
 
-    def segment(n, carry):
-        lax.fori_loop(8 * n, 8 * n + 8, pair, 0)
-        epilogue(4 + n, 0)
-        finished(4 + n)
-        return carry
-
-    lax.fori_loop(0, 4, segment, 0)
-    backward(jnp.int32(unit_count - 2), save[0])
-    backward(jnp.int32(unit_count - 1), save[1])
-
-    for group in range(n_own // 8):
-        for s in range(8):
-            rows = pl.ds(group * 64 + s, 8, stride=8)
-            for k in range(6):
-                ua[k][rows, :] = ub[k][s, group * 8 : group * 8 + 8, :]
-
     def last(step, carry):
         epilogue(step, 0)
         finished(step)
         return carry
 
-    lax.fori_loop(0, 4, last, 0)
-    last(8, 0)
-
-    @pl.when(more)
-    def _():
-        lax.fori_loop(9, TABLE // BATCH, last, 0)
+    lax.fori_loop(0, (unit_count - 2) // 4, pairs, 0)
+    tiled()
+    backward(jnp.int32(unit_count - 2), save[0])
+    backward(jnp.int32(unit_count - 1), save[1])
+    gather_own(1)
+    lax.fori_loop(2, 4, last, 0)
+    last(7, 0)
 
 
 def lane_order(flip):
@@ -520,13 +527,6 @@
             away = jnp.logical_or(rr != r, cc != c)
             op(used(batch, n), away, rr, cc, grads.at[slot], parts.at[k, source], part_send.at[slot], part_recv.at[k, source])
 
-    for slot in range(TILES):
-        cot32[16 * slot : 16 * slot + 16, :] = tiles[slot].astype(jnp.float32)
-
-    compute_kernel(
-        32, plan, landed, lambda batch: partials(ship, batch), table, cot32, kouts, grads, *rest[16:]
-    )
-
     def outputs(op):
         for slot in range(TILES):
             rr, cc, h, k = tile_route(r, c, slot)
@@ -538,7 +538,13 @@
             away = jnp.logical_or(rr != r, cc != c)
             op(go, away, rr, cc, kouts.at[slot], dst, tile_send.at[slot], sem)
 
-    outputs(ship)
+    for slot in range(TILES):
+        cot32[16 * slot : 16 * slot + 16, :] = tiles[slot].astype(jnp.float32)
+
+    compute_kernel(
+        32, plan, landed, lambda batch: partials(ship, batch), lambda: outputs(ship), table, cot32, kouts, grads, *rest[16:]
+    )
+
 
     for h in range(2):
         for k in range(4):
@@ -636,21 +642,22 @@
 def plan():
     r, c = place()
 
+    first = c == 0
+    extras = jnp.where(first, EXTRA, 2)
+
     def unit_of(u):
-        first = c == 0
-        n = u - jnp.where(first, 48, 64)
-        main = n < 0
-        e = jnp.where(n < 2, 2 * c + n, 14 + n)
-        half = jnp.where(r < 8, e // 16, 1 - e // 16)
-        short = jnp.logical_and(first, u < 16)
-        v = jnp.where(first, u + 16, u)
-        slot = jnp.where(main, jnp.where(short, u, v // 2), 32 + n)
-        bb = jnp.where(main, jnp.where(short, 0, v % 2), half)
-        tile = jnp.where(main, bb * 2 + slot // 16, 4 + e // 16)
-        return slot, bb, tile, jnp.where(main, slot, e) % 16
+        v = u - extras
+        main = v >= 0
+        e = jnp.where(u < 2, 2 * c + u, 14 + u)
+        half = jnp.where(r < 8, e >> 4, 1 - (e >> 4))
+        early = v < 32
+        slot = jnp.where(main, jnp.where(early, v, v - jnp.where(first, 16, 32)), 32 + u)
+        bb = jnp.where(main, jnp.where(early, 0, 1), half)
+        tile = jnp.where(main, bb * 2 + (slot >> 4), 4 + (e >> 4))
+        return slot, bb, tile, jnp.where(main, slot, e) & 15
 
     def turned(u):
-        return jnp.where(u < jnp.where(c == 0, 48, 64), r + c >= ROWS, r >= 8)
+        return jnp.where(u < extras, r >= 8, r + c >= ROWS)
 
     return 66, slot_count_of(c), unit_of, turned
 

time: 78.9 us -> 76.4 us (0.968)
  the two profiles are of different devices: /device:TPU:1 before, /device:TPU:97 now
where the time goes in v6:
time: 76.4 us; the launch traced here: 76.2 us
  Pallas kernels  73.4 us (96%)
  local copies, waits for them, and re-layouts  2.13 us (3%)
    pallas_call x1, Pallas kernels, whole_call(): pl.pallas_call(whole_kernel, out_shape=(jax.ShapeDtypeStruct((4, 3072), j...  73.4 us
    unnamed x4, local copies, waits for them, and re-layouts  2.13 us

profile of v6, /device:TPU:97, one launch (start us, length us, event | category | flops | bytes accessed | tf_op | source)
XLA Modules:
  0.0 76.2 jit_solution(13068365784481503116)
XLA Ops:
  0.6 73.4 %shard_map.41 = (f32[4,3072]{1,0:T(4,128)}, f32[2,16,4,16]{3,2,1,0:T(4,128)}) custom-call(bf16[4,3072]{1,0:T(4,128)(2,1)} %bitcast.9, bf16[2,16,4,16]{3,2,1,0:T(4,128)(2,1)} %bitcast.8), custom_call_target="tpu_custom_call" | custom-call | tf_op jit(solution)/shard_map/pallas_call | solution.py:608
  74.0 0.0 copy-start
  74.0 1.5 %copy.5 = f32[4,1,1,3072]{3,2,1,0:T(1,128)} copy(f32[4,1,1,3072]{3,0,2,1:T(4,128)} %bitcast.7) | data formatting | bytes 98304
  75.5 0.0 copy-done
  75.6 0.6 copy.7
Async XLA Ops:
  74.0 1.5 %copy-start = (f32[2,16,4,16]{3,2,1,0:T(4,128)S(1)}, f32[2,16,4,16]{3,2,1,0:T(4,128)}, u32[]{:S(2)}) copy-start(f32[2,16,4,16]{3,2,1,0:T(4,128)} %get-tuple-element.4) | copy-start | bytes 24580

commit v7 on v6

--- a/solution.py
+++ b/solution.py
@@ -347,20 +347,39 @@
 
 def greet(r, c):
     barrier = pltpu.get_barrier_semaphore()
-    x, y, z = (r >> 1) & 3, c >> 1, ((c & 1) << 1) + (r >> 3)
-    xs = [((x + d) & 3) << 1 for d in range(4)]
-    ys = [((y + d) & 3) << 1 for d in range(4)]
-    zs = [((z + d) & 3) for d in range(4)]
-    cores = [r & 1, 1 - (r & 1)]
-    far = lambda o: sum(min(d, 4 - d) for d in o[:3]) + 0.1 * o[3]
-    steps = [(i, j, k, l) for i in range(4) for j in range(4) for k in range(4) for l in range(2)]
-    for i, j, k, l in sorted(steps, key=far, reverse=True)[:-1]:
-        rr = ((zs[k] & 1) << 3) + xs[i] + cores[l]
-        pl.semaphore_signal(barrier, inc=1, device_id=(rr, ys[j] + (zs[k] >> 1)), device_id_type=MESH)
-
-
-def enter():
-    pl.semaphore_wait(pltpu.get_barrier_semaphore(), ROWS * COLS - 1)
+
+    def tell(go, rr, cc):
+        away = jnp.logical_or(rr != r, cc != c)
+        guarded(
+            go, away, lambda: pl.semaphore_signal(barrier, inc=1, device_id=(rr, cc), device_id_type=MESH)
+        )
+
+    for slot in range(66):
+        _, rr, cc, _, _ = partial_route(r, c, slot // BATCH, slot % BATCH)
+        tell(None, rr, cc)
+    rr, cc, _, _ = tile_route(r, c, 4)
+    tell(None, rr, cc)
+
+    @pl.when(c == 0)
+    def _():
+        for slot in range(66, 32 + SLOTS):
+            _, rr, cc, _, _ = partial_route(r, c, slot // BATCH, slot % BATCH)
+            tell(None, rr, cc)
+        rr, cc, _, _ = tile_route(r, c, 5)
+        tell(None, rr, cc)
+
+
+def enter(r, c):
+    count = jnp.int32(0)
+    for _, _, _, _, away in image_routes(r, c):
+        count += 1 if away is None else away.astype(jnp.int32)
+    for k in range(4):
+        dd, _, straight, _, _, _ = cot_route(r, c, 0, k)
+        count += jnp.where(dd == 8, 7 + jnp.where(straight, 0, 1), 0)
+        dd, _, straight, _, _, _ = cot_route(r, c, 1, k)
+        here = jnp.logical_and(straight, c == 0)
+        count += jnp.where(jnp.logical_and(dd == 8, jnp.logical_not(here)), 1, 0)
+    pl.semaphore_wait(pltpu.get_barrier_semaphore(), count)
 
 
 def ship(go, away, rr, cc, src, dst, send_sem, recv_sem):
@@ -487,7 +506,7 @@
             cot32[pl.ds(h * 64 + row, 4, stride=16), 0:16] = part
     for idx in range(8):
         cots[idx] = cot32[16 * idx : 16 * idx + 16, :].astype(jnp.bfloat16)
-    enter()
+    enter(r, c)
 
     def images(op):
         for idx, (k, rr, cc, slot, away) in enumerate(image_routes(r, c)):

time: 76.4 us -> 76.2 us (level)
  no operation moved by 1% of the time
where the time goes in v7:
time: 76.2 us; the launch traced here: 76 us
  Pallas kernels  73.2 us (96%)
  local copies, waits for them, and re-layouts  2.13 us (3%)
    pallas_call x1, Pallas kernels, whole_call(): pl.pallas_call(whole_kernel, out_shape=(jax.ShapeDtypeStruct((4, 3072), j...  73.2 us
    unnamed x4, local copies, waits for them, and re-layouts  2.13 us

profile of v7, /device:TPU:97, one launch (start us, length us, event | category | flops | bytes accessed | tf_op | source)
XLA Modules:
  0.0 76.0 jit_solution(4709715586903805785)
XLA Ops:
  0.6 73.2 %shard_map.41 = (f32[4,3072]{1,0:T(4,128)}, f32[2,16,4,16]{3,2,1,0:T(4,128)}) custom-call(bf16[4,3072]{1,0:T(4,128)(2,1)} %bitcast.9, bf16[2,16,4,16]{3,2,1,0:T(4,128)(2,1)} %bitcast.8), custom_call_target="tpu_custom_call" | custom-call | tf_op jit(solution)/shard_map/pallas_call | solution.py:627
  73.8 0.0 copy-start
  73.8 1.5 %copy.5 = f32[4,1,1,3072]{3,2,1,0:T(1,128)} copy(f32[4,1,1,3072]{3,0,2,1:T(4,128)} %bitcast.7) | data formatting | bytes 98304
  75.3 0.0 copy-done
  75.3 0.6 copy.7
Async XLA Ops:
  73.8 1.5 %copy-start = (f32[2,16,4,16]{3,2,1,0:T(4,128)S(1)}, f32[2,16,4,16]{3,2,1,0:T(4,128)}, u32[]{:S(2)}) copy-start(f32[2,16,4,16]{3,2,1,0:T(4,128)} %get-tuple-element.4) | copy-start | bytes 24580
